TPU v7x, 256 devices: a whole 4x4x8 slice. The times are simulated.
256 devices in a mesh: row: 16 (over y, x), col: 16 (over z, core).
Axes of the slice: x: 4, y: 4, z: 8, core: 2. Of those that a mesh axis runs over, the one named last changes fastest.
Arguments:
- panel: bfloat16 [15, 32, 512, 512], P(None, 'row', 'col'), may hold values from -0.109375 to 0.109375
- diag_inverse: float32 [6, 32, 512, 512], P(None, 'row', 'col'), as said below
- parents: int32 [5, 32], replicated, may hold values from 0 to 31, as said below
- supernode_sizes: int32 [6, 32], replicated, may hold values from 128 to 512
Outputs:
- cross: float32 [15, 32, 512, 512], P(None, 'row', 'col')
- marginal: float32 [6, 32, 512, 512], P(None, 'row', 'col')
Inputs may be any that keep to these rules, and one draw needn't show every extreme that they name: `parents`: the parent of a supernode g of level d + 1 is a supernode of level d whose index divided by 2 equals g divided by 2, or that minus 1 modulo 32 / 2. `diag_inverse`: every block is symmetric and positive definite.
All inputs are finite; a program needn't handle non-finite values.
Results may differ from a plain program's by a relative error of at most 0.0023.
Values may be sent and summed in bfloat16 or wider, within the bound.
A program may use at most 128 MiB of HBM per device.

v0:
```python
import jax
import jax.numpy as jnp
from jax import lax
from jax.sharding import PartitionSpec as P


def from_behind(x, axis, by):
    size = lax.axis_size(axis)
    return lax.ppermute(x, axis, [(i, (i + by) % size) for i in range(size)])


def turn_over(cross):
    swapped = lax.all_to_all(cross, "col", split_axis=3, concat_axis=2, tiled=True)
    return jnp.swapaxes(swapped, 2, 3)


def shards(panel, diag_inverse, parents, supernode_sizes):
    levels = diag_inverse.shape[0]
    per_row = diag_inverse.shape[1]
    row_count = diag_inverse.shape[2]
    width = diag_inverse.shape[3]
    my_row = lax.axis_index("row")
    my_col = lax.axis_index("col")
    my_nodes = my_row * per_row + jnp.arange(per_row, dtype=jnp.int32)
    my_lines = my_col * row_count + jnp.arange(row_count, dtype=jnp.int32)
    columns = jnp.arange(width, dtype=jnp.int32)
    on_diag = (my_lines[:, None] == columns[None, :]).astype(jnp.float32)
    ancestry_ids = jnp.zeros((0, parents.shape[1]), jnp.int32)
    crosses = []
    diagonals = []
    chain = None
    for level in range(levels):
        own_sizes = supernode_sizes[level][my_nodes]
        live_cols = (columns[None, :] < own_sizes[:, None]).astype(jnp.float32)
        live_lines = (my_lines[None, :] < own_sizes[:, None]).astype(jnp.float32)
        diag_base = (
            diag_inverse[level] * live_lines[:, :, None] * live_cols[:, None, :]
            + on_diag[None] * (1.0 - live_lines)[:, :, None]
        )
        if level == 0:
            diagonal = diag_base
        else:
            parent_ids = parents[level - 1]
            ancestry_ids = jnp.concatenate(
                [ancestry_ids[:, parent_ids], parent_ids[None, :]], axis=0
            )
            my_parents = parent_ids[my_nodes]
            pick_slot = jnp.where(
                my_parents // per_row == my_row,
                my_parents % per_row,
                per_row + my_parents % per_row,
            )
            passed = from_behind(chain, "row", 1)
            ancestry = jnp.take(jnp.concatenate([chain, passed], axis=0), pick_slot, axis=0)
            upper_sizes = supernode_sizes[
                jnp.arange(level, dtype=jnp.int32)[:, None], ancestry_ids[:, my_nodes]
            ]
            live_upper = (my_lines[None, None, :] < upper_sizes[:, :, None]).astype(jnp.float32)
            start = level * (level - 1) // 2
            keep = (live_upper[:, :, :, None] * live_cols[None, :, None, :]).astype(jnp.bfloat16)
            lower = jnp.transpose(panel[start : start + level] * keep, (1, 0, 2, 3))
            whole = lax.all_gather(lower, "col", axis=2, tiled=True).astype(jnp.float32)
            cross = -jnp.einsum(
                "nlmik,nmkj->nlij", ancestry, whole, precision=lax.Precision.HIGHEST
            )
            turned = turn_over(cross)
            diagonal = diag_base - jnp.einsum(
                "nlik,nlkj->nij", turned, whole, precision=lax.Precision.HIGHEST
            )
            crosses.append(jnp.transpose(cross, (1, 0, 2, 3)))
        diagonals.append(diagonal)
        if level < levels - 1:
            if level == 0:
                chain = diagonal[:, None, None]
            else:
                upper = jnp.concatenate([ancestry, cross[:, :, None]], axis=2)
                bottom = jnp.concatenate([turned[:, None], diagonal[:, None, None]], axis=2)
                chain = jnp.concatenate([upper, bottom], axis=1)
    return (jnp.concatenate(crosses, axis=0), jnp.stack(diagonals))


def solution(mesh):
    in_specs = (P(None, "row", "col", None), P(None, "row", "col", None), P(), P())
    out_specs = (P(None, "row", "col", None), P(None, "row", "col", None))
    return jax.shard_map(shards, mesh=mesh, in_specs=in_specs, out_specs=out_specs, check_vma=False)
```

profile of v0, /device:TPU:1, one launch (start us, length us, event | category | flops | bytes accessed | tf_op | source)
XLA Modules:
  0.0 466.1 jit_solution(5601063711213045064)
XLA Ops:
  26.2 2.1 collective-permute-start
  28.4 6.0 %collective-permute-done = f32[2,1,1,32,512]{4,3,0,2,1:T(8,128)S(1)} collective-permute-done((f32[2,1,1,32,512]{4,3,0,2,1:T(8,128)S(1)}, f32[2,1,1,32,512]{4,3,0,2,1:T(8,128)S(1)}, u32[]{:S(2)}, u32[]{:S(2)}) %collective-permute-start) | collective-permute-done | bytes 131104 | tf_op jit(solution)/shard_map/ppermute | solution.py:9
  35.0 23.7 %all-gather.15.cloned.1.call-done = bf16[1,2,512,512]{3,2,1,0:T(8,128)(2,1)} async-done(((bf16[1,2,32,512]{3,2,1,0:T(8,128)(2,1)}), bf16[1,2,512,512]{3,2,1,0:T(8,128)(2,1)}) %all-gather.15.cloned.1.call-update) | async-done | bytes 1048592 | tf_op jit(solution)/shard_map/all_gather | solution.py:62
  58.7 2.6 bitcast_dynamic-update-slice_fusion.4
  62.7 4.7 all-to-all-start
  68.8 7.5 %all-to-all-done = f32[16,1,2048]{2,1,0:T(1,128)S(1)} async-done(((f32[16,1,2048]{2,1,0:T(1,128)}), f32[16,1,2048]{2,1,0:T(1,128)S(1)}, u32[]{:S(2)}, u32[]{:S(2)}) %all-to-all-start) | async-done | bytes 131104 | tf_op jit(solution)/shard_map/all_to_all | solution.py:13
  81.4 15.8 %collective-permute-done.1 = f32[2,2,2,32,512]{4,3,0,2,1:T(8,128)S(1)} collective-permute-done((f32[2,2,2,32,512]{4,3,0,2,1:T(8,128)S(1)}, f32[2,2,2,32,512]{4,3,0,2,1:T(8,128)S(1)}, u32[]{:S(2)}, u32[]{:S(2)}) %collective-permute-start.1) | collective-permute-done | bytes 524320 | tf_op jit(solution)/shard_map/ppermute | solution.py:9
  99.0 3.5 bitcast_dynamic-update-slice_fusion.3
  104.9 4.6 all-to-all-start.1
  112.1 11.7 %all-to-all-done.1 = f32[16,1,4096]{2,1,0:T(1,128)S(1)} async-done(((f32[16,1,4096]{2,1,0:T(1,128)}), f32[16,1,4096]{2,1,0:T(1,128)S(1)}, u32[]{:S(2)}, u32[]{:S(2)}) %all-to-all-start.1) | async-done | bytes 262176 | tf_op jit(solution)/shard_map/all_to_all | solution.py:13
  126.9 2.9 copy.212
  131.4 2.7 bitcast_dynamic-update-slice_fusion.7
  138.1 27.5 %collective-permute-done.2 = f32[2,3,3,32,512]{4,3,2,1,0:T(8,128)} collective-permute-done((f32[2,3,3,32,512]{4,3,2,1,0:T(8,128)S(1)}, f32[2,3,3,32,512]{4,3,2,1,0:T(8,128)}, u32[]{:S(2)}, u32[]{:S(2)}) %collective-permute-start.2) | collective-permute-done | bytes 1179680 | tf_op jit(solution)/shard_map/ppermute | solution.py:9
  165.6 3.0 pad_maximum_fusion.2
  168.6 2.3 gather_fusion.12
  171.2 4.3 bitcast_dynamic-update-slice_fusion.2
  176.6 2.3 reshape.1603
  178.9 18.6 %all_to_all.90 = f32[16,1,6144]{2,1,0:T(1,128)S(1)} all-to-all(f32[16,1,6144]{2,1,0:T(1,128)} %reshape.1603), channel_id=1, replica_groups=mesh['row'=16,'col'=16] {'col'}, dimensions={0} | all-to-all | bytes 786432 | tf_op jit(solution)/shard_map/all_to_all | solution.py:13
  197.5 2.4 reduce.8
  199.9 2.3 reshape.1604
  202.2 2.1 copy.211
  206.3 4.1 bitcast_dynamic-update-slice_fusion.6
  212.7 50.0 %collective-permute-done.3 = f32[2,4,4,32,512]{4,3,2,1,0:T(8,128)} collective-permute-done((f32[2,4,4,32,512]{4,3,2,1,0:T(8,128)}, f32[2,4,4,32,512]{4,3,2,1,0:T(8,128)}, u32[]{:S(2)}, u32[]{:S(2)}) %collective-permute-start.3) | collective-permute-done | bytes 2097184 | tf_op jit(solution)/shard_map/ppermute | solution.py:9
  262.7 4.2 pad_maximum_fusion.1
  267.0 4.2 gather_fusion.18
  273.2 4.8 %bitcast_dynamic-update-slice_fusion.1 = (f32[15,2,32,512]{3,2,0,1:T(8,128)}, f32[2,4,32,512]{3,2,1,0:T(8,128)S(1)}) fusion(f32[15,2,32,512]{3,2,0,1:T(8,128)} %get-tuple-element.48, f32[2,4,4,32,512]{4,3,2,1,0:T(8,128)S(1)} %broadcast_select_fusion, bf16[2,4,512,512]{3,2,1,0:T(8,128)(2,1)} %all-gather.11.cloned.1.call-done), kind=kOutput, calls=%fused_computation.81 | convolution fusion | flops 3221356544 | bytes 7340032 | tf_op jit(solution)/shard_map/nlmik,nmkj->nlij/dot_general | solution.py:63
  279.8 2.8 reshape.1605
  282.6 21.3 %all_to_all.91 = f32[16,1,8192]{2,1,0:T(1,128)} all-to-all(f32[16,1,8192]{2,1,0:T(1,128)S(1)} %reshape.1605), channel_id=1, replica_groups=mesh['row'=16,'col'=16] {'col'}, dimensions={0} | all-to-all | bytes 1048576 | tf_op jit(solution)/shard_map/all_to_all | solution.py:13
  303.9 2.9 reduce.9
  306.8 2.5 reshape.1606
  309.3 4.1 copy.210
  313.4 2.3 all_to_all.80
  315.7 4.9 %bitcast_dynamic-update-slice_fusion.5 = (f32[6,2,32,512]{3,2,1,0:T(8,128)}, f32[2,32,512]{2,1,0:T(8,128)S(1)}) fusion(f32[6,2,32,512]{3,2,1,0:T(8,128)} %get-tuple-element.58, bf16[2,4,512,512]{3,2,1,0:T(8,128)(2,1)} %all-gather.11.cloned.1.call-done, f32[2,4,512,32]{2,3,1,0:T(8,128)S(1)} %all_to_all.80, f32[2,32]{1,0:T(2,128)S(1)} %get-tuple-element.39, ...), kind=kOutput, calls=%fused_computation.105 | convolution fusion | flops 805470208 | bytes 5181952 | tf_op jit(solution)/shard_map/nlik,nlkj->nij/dot_general | solution.py:67
  320.6 2.1 maximum_maximum_fusion
  323.6 74.8 %collective-permute-done.4 = f32[2,5,5,32,512]{4,3,2,1,0:T(8,128)} collective-permute-done((f32[2,5,5,32,512]{4,3,2,1,0:T(8,128)}, f32[2,5,5,32,512]{4,3,2,1,0:T(8,128)}, u32[]{:S(2)}, u32[]{:S(2)}) %collective-permute-start.4) | collective-permute-done | bytes 3276832 | tf_op jit(solution)/shard_map/ppermute | solution.py:9
  398.4 4.7 %pad_maximum_fusion = f32[4,5,5,32,512]{4,3,2,1,0:T(8,128)} fusion(f32[2,5,5,32,512]{4,3,2,1,0:T(8,128)} %collective-permute-done.4, f32[2,1,1,32,512]{4,3,2,1,0:T(8,128)S(1)} %bitcast.445, f32[2,1,4,32,512]{4,3,2,1,0:T(8,128)S(1)} %bitcast.421, f32[2,4,1,32,512]{4,3,2,1,0:T(8,128)S(1)} %bitcast.436, f32[2,4,4,32,512]{4,3,2,1,0:T(8,128)S(1)} %broadcast_select_fusion), kind=kLoop, calls=%fused_computation.30 | loop fusion | flops 6553600 | bytes 13107200 | tf_op jit(solution)/shard_map/concatenate | solution.py:54
  403.1 3.6 gather_fusion.24
  406.8 6.4 %bitcast_dynamic-update-slice_fusion = (f32[15,2,32,512]{3,2,0,1:T(8,128)}, f32[2,5,32,512]{3,2,1,0:T(8,128)}) fusion(f32[15,2,32,512]{3,2,0,1:T(8,128)} %get-tuple-element.50, bf16[2,5,512,512]{3,2,1,0:T(8,128)(2,1)} %all-gather.13.cloned.1.call-done, f32[2,5,5,32,512]{4,3,2,1,0:T(8,128)S(1)} %gather_fusion.24, pred[2]{0:T(512)(128)(4,1)S(1)} %compare_and_fusion), kind=kOutput, calls=%fused_computation.76 | convolution fusion | flops 5034147840 | bytes 9830402 | tf_op jit(solution)/shard_map/nlmik,nmkj->nlij/dot_general | solution.py:63
  413.1 3.1 copy.173
  416.2 3.4 reshape.1607
  419.6 4.3 all-to-all-start.4
  423.9 3.1 copy.175
  426.9 16.8 %all-to-all-done.4 = f32[16,1,10240]{2,1,0:T(1,128)S(1)} async-done(((f32[16,1,10240]{2,1,0:T(1,128)}), f32[16,1,10240]{2,1,0:T(1,128)S(1)}, u32[]{:S(2)}, u32[]{:S(2)}) %all-to-all-start.4) | async-done | bytes 655392 | tf_op jit(solution)/shard_map/all_to_all | solution.py:13
  443.7 2.2 reduce.10
  445.9 2.2 reshape.1608
  448.1 3.1 copy.209
  451.2 2.5 all_to_all.84
  453.6 5.7 %fusion.43 = f32[6,2,32,512]{3,2,1,0:T(8,128)} fusion(f32[6,2,32,512]{3,2,1,0:T(8,128)} %get-tuple-element.60, bf16[2,5,512,512]{3,2,1,0:T(8,128)(2,1)} %all-gather.13.cloned.1.call-done, f32[2,5,512,32]{2,3,1,0:T(8,128)S(1)} %all_to_all.84, f32[6,2,32,512]{3,2,1,0:T(8,128)} %param.5, f32[2,32]{1,0:T(2,128)S(1)} %get-tuple-element.38, ...), kind=kOutput, calls=%fused_computation.67 | convolution fusion | flops 1006796800 | bytes 6230528 | tf_op jit(solution)/shard_map/nlik,nlkj->nij/dot_general | solution.py:67
  (155 shorter events, 53.2 us)
Async XLA Ops:
  7.2 8.7 %copy-start.5 = (s32[5,32]{1,0:T(8,128)S(1)}, s32[5,32]{1,0:T(8,128)}, u32[]{:S(2)}) copy-start(s32[5,32]{1,0:T(8,128)} %param.6) | copy-start | bytes 1924
  7.2 7.9 %copy-start.4 = (bf16[15,2,32,512]{3,2,1,0:T(8,128)(2,1)S(1)}, bf16[15,2,32,512]{3,2,1,0:T(8,128)(2,1)}, u32[]{:S(2)}) copy-start(bf16[15,2,32,512]{3,2,1,0:T(8,128)(2,1)} %param.4) | copy-start | bytes 2949124
  7.2 51.5 %all-gather.15.cloned.1.call-start = ((), (), s32[]{:S(2)}) async-start(), calls=%async_computation.9 | async-start | bytes 1114112 | tf_op jit(solution)/shard_map/all_gather | solution.py:62
  8.8 8.6 %copy-start = (s32[6,32]{1,0:T(8,128)S(1)}, s32[6,32]{1,0:T(8,128)}, u32[]{:S(2)}) copy-start(s32[6,32]{1,0:T(8,128)} %param.7) | copy-start | bytes 2308
  15.8 83.2 %all-gather.7.cloned.1.call-start = ((), (), s32[]{:S(2)}) async-start(), calls=%async_computation.5 | async-start | bytes 2228224 | tf_op jit(solution)/shard_map/all_gather | solution.py:62
  19.2 152.0 %all-gather.9.cloned.1.call-start = ((), (), s32[]{:S(2)}) async-start(), calls=%async_computation.6 | async-start | bytes 3342336 | tf_op jit(solution)/shard_map/all_gather | solution.py:62
  21.3 4.8 %copy-start.3 = (f32[6,2,32,512]{3,2,1,0:T(8,128)S(1)}, f32[6,2,32,512]{3,2,1,0:T(8,128)}, u32[]{:S(2)}) copy-start(f32[6,2,32,512]{3,2,1,0:T(8,128)} %param.5) | copy-start | bytes 2359300
  22.5 250.7 %all-gather.11.cloned.1.call-start = ((), (), s32[]{:S(2)}) async-start(), calls=%async_computation.7 | async-start | bytes 4456448 | tf_op jit(solution)/shard_map/all_gather | solution.py:62
  26.2 8.2 %collective-permute-start = (f32[2,1,1,32,512]{4,3,0,2,1:T(8,128)S(1)}, f32[2,1,1,32,512]{4,3,0,2,1:T(8,128)S(1)}, u32[]{:S(2)}, u32[]{:S(2)}) collective-permute-start(f32[2,1,1,32,512]{4,3,0,2,1:T(8,128)S(1)} %fusion.71), channel_id=1, source_target_pairs={{0,16},{16,32},{32,48},{48,64},{64,80},{80,96},{96,112},{112,128},... | collective-permute-start | bytes 393224 | tf_op jit(solution)/shard_map/ppermute | solution.py:9
  61.5 17.4 %copy-start.2 = (bf16[1,2,512,512]{3,2,1,0:T(8,128)(2,1)S(1)}, bf16[1,2,512,512]{3,2,1,0:T(8,128)(2,1)}, u32[]{:S(2)}) copy-start(bf16[1,2,512,512]{3,2,1,0:T(8,128)(2,1)} %all-gather.15.cloned.1.call-done) | copy-start | bytes 3145732
  62.7 13.6 %all-to-all-start = ((f32[16,1,2048]{2,1,0:T(1,128)}), f32[16,1,2048]{2,1,0:T(1,128)S(1)}, u32[]{:S(2)}, u32[]{:S(2)}) async-start(f32[16,1,2048]{2,1,0:T(1,128)} %reshape.1599), calls=%async_computation | async-start | bytes 262144 | tf_op jit(solution)/shard_map/all_to_all | solution.py:13
  80.1 17.1 %collective-permute-start.1 = (f32[2,2,2,32,512]{4,3,0,2,1:T(8,128)S(1)}, f32[2,2,2,32,512]{4,3,0,2,1:T(8,128)S(1)}, u32[]{:S(2)}, u32[]{:S(2)}) collective-permute-start(f32[2,2,2,32,512]{4,3,0,2,1:T(8,128)S(1)} %maximum_maximum_fusion.3), channel_id=1, source_target_pairs={{0,16},{16,32},{32,48},{48,64},{64,80},{80,96},{96,112},{112,128},... | collective-permute-start | bytes 1572872 | tf_op jit(solution)/shard_map/ppermute | solution.py:9
  104.9 18.8 %all-to-all-start.1 = ((f32[16,1,4096]{2,1,0:T(1,128)}), f32[16,1,4096]{2,1,0:T(1,128)S(1)}, u32[]{:S(2)}, u32[]{:S(2)}) async-start(f32[16,1,4096]{2,1,0:T(1,128)} %reshape.1601), calls=%async_computation.1 | async-start | bytes 524288 | tf_op jit(solution)/shard_map/all_to_all | solution.py:13
  109.5 297.3 %all-gather.13.cloned.1.call-start = ((), (), s32[]{:S(2)}) async-start(), calls=%async_computation.8 | async-start | bytes 5570560 | tf_op jit(solution)/shard_map/all_gather | solution.py:62
  125.0 6.4 %copy-start.1 = (bf16[2,2,512,512]{3,2,1,0:T(8,128)(2,1)S(1)}, bf16[2,2,512,512]{3,2,1,0:T(8,128)(2,1)}, u32[]{:S(2)}) copy-start(bf16[2,2,512,512]{3,2,1,0:T(8,128)(2,1)} %all-gather.7.cloned.1.call-done) | copy-start | bytes 6291460
  134.2 31.4 %collective-permute-start.2 = (f32[2,3,3,32,512]{4,3,2,1,0:T(8,128)S(1)}, f32[2,3,3,32,512]{4,3,2,1,0:T(8,128)}, u32[]{:S(2)}, u32[]{:S(2)}) collective-permute-start(f32[2,3,3,32,512]{4,3,2,1,0:T(8,128)S(1)} %maximum_maximum_fusion.2), channel_id=1, source_target_pairs={{0,16},{16,32},{32,48},{48,64},{64,80},{80,96},{96,112},{112,128},... | collective-permute-start | bytes 3538952 | tf_op jit(solution)/shard_map/ppermute | solution.py:9
  212.0 50.7 %collective-permute-start.3 = (f32[2,4,4,32,512]{4,3,2,1,0:T(8,128)}, f32[2,4,4,32,512]{4,3,2,1,0:T(8,128)}, u32[]{:S(2)}, u32[]{:S(2)}) collective-permute-start(f32[2,4,4,32,512]{4,3,2,1,0:T(8,128)} %maximum_maximum_fusion.1), channel_id=1, source_target_pairs={{0,16},{16,32},{32,48},{48,64},{64,80},{80,96},{96,112},{112,128},... | collective-permute-start | bytes 6291464 | tf_op jit(solution)/shard_map/ppermute | solution.py:9
  322.7 75.7 %collective-permute-start.4 = (f32[2,5,5,32,512]{4,3,2,1,0:T(8,128)}, f32[2,5,5,32,512]{4,3,2,1,0:T(8,128)}, u32[]{:S(2)}, u32[]{:S(2)}) collective-permute-start(f32[2,5,5,32,512]{4,3,2,1,0:T(8,128)} %maximum_maximum_fusion), channel_id=1, source_target_pairs={{0,16},{16,32},{32,48},{48,64},{64,80},{80,96},{96,112},{112,128},... | collective-permute-start | bytes 9830408 | tf_op jit(solution)/shard_map/ppermute | solution.py:9
  419.6 24.1 %all-to-all-start.4 = ((f32[16,1,10240]{2,1,0:T(1,128)}), f32[16,1,10240]{2,1,0:T(1,128)S(1)}, u32[]{:S(2)}, u32[]{:S(2)}) async-start(f32[16,1,10240]{2,1,0:T(1,128)} %reshape.1607), calls=%async_computation.4 | async-start | bytes 1310720 | tf_op jit(solution)/shard_map/all_to_all | solution.py:13
Sparse Core Ops, SparseCore 0:
  15.9 42.7 all-gather.14
  60.5 38.4 all-gather.6
  100.9 42.6 all-gather.8
  145.3 41.1 all-gather.10
  188.2 47.3 all-gather.12
where the time goes:
time: 474 us; the launch traced here: 466 us
  waiting for transfers between devices  235 us (50%)
  local copies, waits for them, and re-layouts  82.8 us (17%)
  matrix products  40.3 us (9%)
  blocking collectives  39.9 us (8%)
  other arithmetic  35.3 us (7%)
  starting transfers between devices  18.6 us (4%)
  between operations  14.5 us (3%)
    ppermute x5, waiting for transfers between devices, from_behind(): return lax.ppermute(x, axis, [(i, (i + by) % size) for i in range(size)])  174 us
    all_to_all x2, blocking collectives, turn_over(): lax.all_to_all(cross, 'col', split_axis=3, concat_axis=2, tiled=True)  39.9 us
    all_to_all x3, waiting for transfers between devices, turn_over(): lax.all_to_all(cross, 'col', split_axis=3, concat_axis=2, tiled=True)  35.9 us
    all_gather x5, waiting for transfers between devices, shards(): whole = lax.all_gather(lower, 'col', axis=2, tiled=True).astype(jnp.float32)  24.7 us
    unnamed x26, local copies, waits for them, and re-layouts  24.1 us
    all_to_all x11, local copies, waits for them, and re-layouts, turn_over(): lax.all_to_all(cross, 'col', split_axis=3, concat_axis=2, tiled=True)  21.7 us
    dot_general x5, matrix products, shards(): jnp.einsum('nlmik,nmkj->nlij', ancestry, whole, precision=lax.Precision.H...  21.6 us
    dot_general x5, matrix products, shards(): jnp.einsum('nlik,nlkj->nij', turned, whole, precision=lax.Precision.HIGHEST)  18.7 us
  transfers between devices with their start and end apart: 13, of which 10 were waited for; matrix products, arithmetic and copies ran while one was open for 25% of the time, Pallas kernels for 0%

commit v1 on v0

v1 whole, which is shorter than its diff:
```python
import functools

import jax
import jax.numpy as jnp
from jax import lax
from jax.experimental import pallas as pl
from jax.experimental.pallas import tpu as pltpu
from jax.sharding import PartitionSpec as P

MESH = pl.DeviceIdType.MESH
LEVELS = 6
F32 = jnp.float32
BF16 = jnp.bfloat16


def lanes_of(level):
    return 128 * (-(-32 * level // 128))


def kernel(rows_n, cols_n, panel, diag, parents, sizes, cross_out, marg_out, *scratch):
    cands = scratch[0:5]
    fulls = scratch[5:10]
    turn_out = scratch[10:15]
    turn_in = scratch[15:20]
    lhs, acc, ring_send, ring_recv, mate_send, mate_recv, chain_send, chain_recv, turn_send, turn_recv = scratch[20:]
    width = diag.shape[3]
    lines = diag.shape[2]
    chips = cols_n // 2
    row = lax.axis_index("row")
    col = lax.axis_index("col")
    chip = col // 2
    core = col % 2
    mate = col + 1 - 2 * core
    right = (col + 2) % cols_n
    left = (col + cols_n - 2) % cols_n
    next_row = (row + 1) % rows_n
    prev_row = (row + rows_n - 1) % rows_n

    barrier = pltpu.get_barrier_semaphore()
    for k in range(1, cols_n):
        pl.semaphore_signal(barrier, inc=1, device_id=(row, (col + k) % cols_n), device_id_type=MESH)
    pl.semaphore_signal(barrier, inc=1, device_id=(next_row, col), device_id_type=MESH)
    pl.semaphore_signal(barrier, inc=1, device_id=(prev_row, col), device_id_type=MESH)
    pl.semaphore_wait(barrier, cols_n + 1)

    line_of = lax.broadcasted_iota(jnp.int32, (lines, width), 0) + col * lines
    column_of = lax.broadcasted_iota(jnp.int32, (lines, width), 1)

    def base_of(level, n):
        size = sizes[level, row * 2 + n]
        live = (line_of < size) & (column_of < size)
        eye = (line_of == column_of) & (line_of >= size)
        return jnp.where(live, diag[level, n], jnp.where(eye, 1.0, 0.0))

    def strip(level, at, first, count):
        return fulls[level - 1].at[
            pl.ds(first, count), pl.ds(pl.multiple_of(at * lines, lines), lines), :
        ]

    def share(level, way, step):
        if step < 3:
            return 0, 2 * level
        return (0, level) if way == 0 else (level, level)

    def ring_copy(level, way, step, arriving):
        hop = step + 1 if arriving else step
        at = ((chip - hop + chips) % chips if way == 0 else (chip + hop) % chips) * 2 + core
        piece = strip(level, at, *share(level, way, step))
        return pltpu.make_async_remote_copy(
            src_ref=piece, dst_ref=piece,
            send_sem=ring_send.at[level - 1, way, step],
            recv_sem=ring_recv.at[level - 1, way, step],
            device_id=(row, right if way == 0 else left), device_id_type=MESH,
        )

    def mate_copy(level, index, arriving):
        whose = 1 - core if arriving else core
        if index == 0:
            at, part = chip, (0, 2 * level)
        else:
            way, step = (index - 1) // 4, (index - 1) % 4
            at = (chip - step - 1 + chips) % chips if way == 0 else (chip + step + 1) % chips
            part = share(level, way, step)
        piece = strip(level, at * 2 + whose, *part)
        return pltpu.make_async_remote_copy(
            src_ref=piece, dst_ref=piece,
            send_sem=mate_send.at[level - 1, index],
            recv_sem=mate_recv.at[level - 1, index],
            device_id=(row, mate), device_id_type=MESH,
        )

    def mask_factor(level):
        start = level * (level - 1) // 2

        def one(n, _):
            node = row * 2 + n
            size = sizes[level, node]
            above = node
            for up in range(level - 1, -1, -1):
                above = parents[up, above]
                upper = sizes[up, above]
                keep = (line_of < upper) & (column_of < size)
                block = jnp.where(keep, panel[start + up, n].astype(F32), 0.0)
                fulls[level - 1][
                    n * level + up, pl.ds(pl.multiple_of(col * lines, lines), lines), :
                ] = block.astype(BF16)
            return 0

        lax.fori_loop(0, 2, one, 0)

    def ring(level, step):
        for way in (0, 1):
            if step > 0:
                ring_copy(level, way, step - 1, True).wait_recv()
            if step < 4:
                ring_copy(level, way, step, False).start()
        if step == 0:
            mate_copy(level, 0, False).start()
        else:
            mate_copy(level, step, False).start()
            mate_copy(level, 4 + step, False).start()

    def ring_end(level):
        for index in range(9):
            mate_copy(level, index, True).wait_recv()

    def chain_part(level, n, part, there):
        d = level
        first, count = ((0, d * d), (d * d, d), (d * d + d, d), (d * d + 2 * d, 1))[part]
        return cands[d].at[n + 2 if there else n, pl.ds(first, count)]

    def chain_copy(level, n, part):
        return pltpu.make_async_remote_copy(
            src_ref=chain_part(level, n, part, False),
            dst_ref=chain_part(level, n, part, True),
            send_sem=chain_send.at[level, n, part],
            recv_sem=chain_recv.at[level, n, part],
            device_id=(next_row, col), device_id_type=MESH,
        )

    def turn_copy(level, n, k):
        there = (col + k) % cols_n
        return pltpu.make_async_remote_copy(
            src_ref=turn_out[level - 1].at[n, there],
            dst_ref=turn_in[level - 1].at[n, col],
            send_sem=turn_send.at[level - 1, n, k],
            recv_sem=turn_recv.at[level - 1, n, k],
            device_id=(row, there), device_id_type=MESH,
        )

    def turn_arrival(level, n, k):
        whence = (col + cols_n - k) % cols_n
        return pltpu.make_async_remote_copy(
            src_ref=turn_out[level - 1].at[n, whence],
            dst_ref=turn_in[level - 1].at[n, whence],
            send_sem=turn_send.at[level - 1, n, k],
            recv_sem=turn_recv.at[level - 1, n, k],
            device_id=(row, whence), device_id_type=MESH,
        )

    def parts_of(level):
        return (3,) if level == 0 else (0, 1, 2, 3)

    def split(value):
        high = value.astype(BF16)
        return high, (value - high.astype(F32)).astype(BF16)

    def select_and_cross(level):
        d = level - 1
        start = level * (level - 1) // 2
        tall = lines * level

        def one(n, _):
            node = row * 2 + n
            parent = parents[d, node]
            own = (parent >= row * 2) & (parent < row * 2 + 2)
            slot = jnp.where(own, 0, 2) + lax.rem(parent, 2)
            for l in range(level):
                for m in range(level):
                    if l < d and m < d:
                        entry = l * d + m
                    elif l < d:
                        entry = d * d + l
                    elif m < d:
                        entry = d * d + d + m
                    else:
                        entry = d * d + 2 * d
                    value = cands[d][slot, entry]
                    if level < LEVELS - 1:
                        cands[level][n, l * level + m] = value
                    high, low = split(value)
                    lhs[m, l * lines : (l + 1) * lines, :] = high
                    lhs[m, tall + l * lines : tall + (l + 1) * lines, :] = low
            if level < LEVELS - 1:
                chain_copy(level, n, 0).start()
            acc[0 : 2 * tall, :] = jnp.zeros((2 * tall, width), F32)

            def add(m, _):
                acc[0 : 2 * tall, :] += jnp.dot(
                    lhs[m, 0 : 2 * tall, :], fulls[level - 1][n * level + m], preferred_element_type=F32
                )
                return 0

            lax.fori_loop(0, level, add, 0)
            crossed = -(acc[0:tall, :] + acc[tall : 2 * tall, :])
            for l in range(level):
                piece = crossed[l * lines : (l + 1) * lines, :]
                cross_out[start + l, n] = piece
                if level < LEVELS - 1:
                    cands[level][n, level * level + l] = piece
            if level < LEVELS - 1:
                chain_copy(level, n, 1).start()
            turned = jnp.transpose(crossed, (1, 0))
            for c in range(cols_n):
                turn_out[level - 1][n, c, :, 0:tall] = turned[c * lines : (c + 1) * lines, :]

            def send(k, _):
                turn_copy(level, n, k).start()
                return 0

            lax.fori_loop(1, cols_n, send, 0)
            turn_in[level - 1][n, col] = turn_out[level - 1][n, col]
            return 0

        lax.fori_loop(0, 2, one, 0)

    lane_of = lax.broadcasted_iota(jnp.int32, (lines, 128), 1)
    per = 128 // lines

    def finish_level(level):
        def one(n, _):
            def arrive(k, _):
                turn_arrival(level, n, k).wait_recv()
                return 0

            lax.fori_loop(1, cols_n, arrive, 0)
            for l in range(level):
                for q in range(width // 128):
                    piece = None
                    for k in range(per):
                        source = turn_in[level - 1][
                            n, q * per + k, :, (l // per) * 128 : (l // per) * 128 + 128
                        ]
                        shift = ((k - l % per) * lines) % 128
                        if shift:
                            source = pltpu.roll(source, shift, 1)
                        piece = source if piece is None else jnp.where(lane_of >= k * lines, source, piece)
                    high, low = split(piece)
                    lhs[l, 0:lines, q * 128 : (q + 1) * 128] = high
                    lhs[l, lines : 2 * lines, q * 128 : (q + 1) * 128] = low
                    if level < LEVELS - 1:
                        cands[level][n, level * level + level + l, :, q * 128 : (q + 1) * 128] = piece
            if level < LEVELS - 1:
                chain_copy(level, n, 2).start()
            acc[0 : 2 * lines, :] = jnp.zeros((2 * lines, width), F32)

            def add(l, _):
                acc[0 : 2 * lines, :] += jnp.dot(
                    lhs[l, 0 : 2 * lines, :], fulls[level - 1][n * level + l], preferred_element_type=F32
                )
                return 0

            lax.fori_loop(0, level, add, 0)
            marginal = base_of(level, n) - (acc[0:lines, :] + acc[lines : 2 * lines, :])
            marg_out[level, n] = marginal
            if level < LEVELS - 1:
                cands[level][n, level * level + 2 * level] = marginal
                chain_copy(level, n, 3).start()
            return 0

        lax.fori_loop(0, 2, one, 0)

    mask_factor(1)
    ring(1, 0)
    for n in range(2):
        marginal = base_of(0, n)
        marg_out[0, n] = marginal
        cands[0][n, 0] = marginal
        chain_copy(0, n, 3).start()
    mask_factor(2)
    ring(2, 0)
    ring(1, 1)
    mask_factor(3)
    ring(2, 1)
    ring(1, 2)
    mask_factor(4)
    ring(2, 2)
    ring(1, 3)
    mask_factor(5)
    ring(2, 3)
    ring(3, 0)
    ring(1, 4)
    before = {1: (), 2: ((2, 4),), 3: ((3, 4),), 4: ((4, 4),), 5: ((5, 4),)}
    middle = {1: ((3, 1), (3, 2)), 2: ((4, 0), (4, 1)), 3: ((5, 1), (5, 2)), 4: (), 5: ()}
    after = {1: ((3, 3),), 2: ((4, 2), (4, 3), (5, 0)), 3: ((5, 3),), 4: (), 5: ()}
    for level in range(1, LEVELS):
        for job in before[level]:
            ring(*job)
        ring_end(level)
        for n in range(2):
            for part in parts_of(level - 1):
                chain_copy(level - 1, n, part).wait_recv()
        select_and_cross(level)
        for job in middle[level]:
            ring(*job)
        finish_level(level)
        for job in after[level]:
            ring(*job)

    for level in range(1, LEVELS):
        for way in (0, 1):
            for step in range(4):
                ring_copy(level, way, step, False).wait_send()
        for index in range(9):
            mate_copy(level, index, False).wait_send()

        def sent(k, _):
            turn_copy(level, 0, k).wait_send()
            turn_copy(level, 1, k).wait_send()
            return 0

        lax.fori_loop(1, cols_n, sent, 0)
    for level in range(LEVELS - 1):
        for n in range(2):
            for part in parts_of(level):
                chain_copy(level, n, part).wait_send()


def solution(mesh):
    rows_n, cols_n = mesh.shape["row"], mesh.shape["col"]

    def shards(panel, diag_inverse, parents, sizes):
        pairs, per, lines, width = panel.shape
        vmem = pl.BlockSpec(memory_space=pltpu.VMEM)
        smem = pl.BlockSpec(memory_space=pltpu.SMEM)
        dma = pltpu.SemaphoreType.DMA
        return pl.pallas_call(
            functools.partial(kernel, rows_n, cols_n),
            out_shape=(
                jax.ShapeDtypeStruct((pairs, per, lines, width), F32),
                jax.ShapeDtypeStruct((LEVELS, per, lines, width), F32),
            ),
            in_specs=[vmem, vmem, smem, smem],
            out_specs=(vmem, vmem),
            scratch_shapes=[
                *[pltpu.VMEM((4, (d + 1) * (d + 1), lines, width), F32) for d in range(5)],
                *[pltpu.VMEM((2 * d, width, width), BF16) for d in range(1, 6)],
                *[pltpu.VMEM((2, cols_n, lines, lanes_of(d)), F32) for d in range(1, 6)],
                *[pltpu.VMEM((2, cols_n, lines, lanes_of(d)), F32) for d in range(1, 6)],
                pltpu.VMEM((5, 320, width), BF16),
                pltpu.VMEM((320, width), F32),
                dma((5, 2, 4)),
                dma((5, 2, 4)),
                dma((5, 9)),
                dma((5, 9)),
                dma((5, 2, 4)),
                dma((5, 2, 4)),
                dma((5, 2, cols_n)),
                dma((5, 2, cols_n)),
            ],
            compiler_params=pltpu.CompilerParams(
                collective_id=0, has_side_effects=True, vmem_limit_bytes=64000 * 1024
            ),
        )(panel, diag_inverse, parents, sizes)

    in_specs = (P(None, "row", "col", None), P(None, "row", "col", None), P(), P())
    out_specs = (P(None, "row", "col", None), P(None, "row", "col", None))
    return jax.shard_map(shards, mesh=mesh, in_specs=in_specs, out_specs=out_specs, check_vma=False)
```

time: 474 us -> 255 us (0.54); the launches traced: 466 us -> 255 us
  Pallas kernels: 0 us -> 250 us
  waiting for transfers between devices: 235 us -> 0 us
  local copies, waits for them, and re-layouts: 82.8 us -> 4.03 us
  matrix products: 40.3 us -> 0 us
  blocking collectives: 39.9 us -> 0 us
  other arithmetic: 35.3 us -> 0 us
  starting transfers between devices: 18.6 us -> 0 us
  between operations: 14.5 us -> 0.65 us
    pallas_call x0 -> x1, Pallas kernels: none -> 250 us  [shards(): pl.pallas_call(functools.partial(kernel, rows_n, cols_n), out_shape=(jax....]
    ppermute x5 -> x0, waiting for transfers between devices: 174 us -> none  [from_behind(): return lax.ppermute(x, axis, [(i, (i + by) % size) for i in range(size)])]
    dot_general x10 -> x0, matrix products: 40.3 us -> none  [the longest x5 21.6 us: shards(): jnp.einsum('nlmik,nmkj->nlij', ancestry, whole, precision=lax.Precision.H...]
    all_to_all x2 -> x0, blocking collectives: 39.9 us -> none  [turn_over(): lax.all_to_all(cross, 'col', split_axis=3, concat_axis=2, tiled=True)]
    all_to_all x3 -> x0, waiting for transfers between devices: 35.9 us -> none  [turn_over(): lax.all_to_all(cross, 'col', split_axis=3, concat_axis=2, tiled=True)]
    gather x38 -> x0, local copies, waits for them, and re-layouts: 27.7 us -> none  [the longest x5 11.3 us: shards(): jnp.take(jnp.concatenate([chain, passed], axis=0), pick_slot, axis=0)]
    all_gather x5 -> x0, waiting for transfers between devices: 24.7 us -> none  [shards(): whole = lax.all_gather(lower, 'col', axis=2, tiled=True).astype(jnp.float32)]
    all_to_all x11 -> x0, local copies, waits for them, and re-layouts: 21.7 us -> none  [turn_over(): lax.all_to_all(cross, 'col', split_axis=3, concat_axis=2, tiled=True)]
  transfers between devices with their start and end apart: 13 -> 0, of which waited for: 10 -> 0; matrix products, arithmetic and copies ran while one was open for 25% -> 0% of each run, Pallas kernels for 0% -> 0%
where the time goes in v1:
time: 255 us
  Pallas kernels  250 us (98%)
  local copies, waits for them, and re-layouts  4.03 us (2%)
    pallas_call x1, Pallas kernels, shards(): pl.pallas_call(functools.partial(kernel, rows_n, cols_n), out_shape=(jax....  250 us

profile of v1, /device:TPU:1, one launch (start us, length us, event | category | flops | bytes accessed | tf_op | source)
XLA Modules:
  0.0 254.7 jit_solution(13999386883192800889)
XLA Ops:
  0.6 250.1 %shard_map.59 = (f32[15,2,32,512]{3,2,1,0:T(8,128)}, f32[6,2,32,512]{3,2,1,0:T(8,128)}) custom-call(bf16[15,2,32,512]{3,2,1,0:T(8,128)(2,1)} %panel.1, f32[6,2,32,512]{3,2,1,0:T(8,128)} %diag.1, s32[5,32]{1,0:T(8,128)} %parents.1, s32[6,32]{1,0:T(8,128)} %sizes.1), custom_call_target="tpu_custom_call" | custom-call | tf_op jit(solution)/shard_map/pallas_call | solution.py:337
  250.7 0.0 copy-start
  250.7 3.1 %copy.8 = f32[15,2,32,512]{3,2,1,0:T(8,128)} copy(f32[15,2,32,512]{3,2,1,0:T(8,128)} %get-tuple-element.4) | data formatting | bytes 3932160
  253.9 0.0 copy-done
  253.9 0.9 copy.9
Async XLA Ops:
  250.7 3.2 %copy-start = (f32[6,2,32,512]{3,2,1,0:T(8,128)S(1)}, f32[6,2,32,512]{3,2,1,0:T(8,128)}, u32[]{:S(2)}) copy-start(f32[6,2,32,512]{3,2,1,0:T(8,128)} %get-tuple-element.5) | copy-start | bytes 2359300

commit v2 on v1

--- a/solution.py
+++ b/solution.py
@@ -13,8 +13,32 @@
 BF16 = jnp.bfloat16
 
 
+POWER = 6
+
+
+def joint(level):
+    return level <= 2
+
+
 def lanes_of(level):
-    return 128 * (-(-32 * level // 128))
+    tall = 32 * level * (2 if joint(level) else 1)
+    return 128 * (-(-tall // 128))
+
+
+def scale_of(value):
+    top = jnp.max(jnp.max(jnp.abs(value), axis=0, keepdims=True), axis=1, keepdims=True)
+    return jnp.maximum(top, 1e-30).astype(BF16).astype(F32)
+
+
+def encode(value, scale):
+    unit = value * (1.0 / scale)
+    square = unit * unit
+    return unit * jnp.abs(unit) * (square * square)
+
+
+def decode(code):
+    root = jnp.exp(jnp.log(jnp.abs(code)) * (1.0 / POWER))
+    return jnp.where(code > 0.0, root, jnp.where(code < 0.0, -root, 0.0))
 
 
 def kernel(rows_n, cols_n, panel, diag, parents, sizes, cross_out, marg_out, *scratch):
@@ -22,7 +46,11 @@
     fulls = scratch[5:10]
     turn_out = scratch[10:15]
     turn_in = scratch[15:20]
-    lhs, acc, ring_send, ring_recv, mate_send, mate_recv, chain_send, chain_recv, turn_send, turn_recv = scratch[20:]
+    scales = scratch[20:25]
+    (
+        lhs, acc, opened, turned_f32, ring_send, ring_recv, mate_send, mate_recv,
+        chain_send, chain_recv, scale_send, scale_recv, turn_send, turn_recv,
+    ) = scratch[25:]
     width = diag.shape[3]
     lines = diag.shape[2]
     chips = cols_n // 2
@@ -57,35 +85,32 @@
             pl.ds(first, count), pl.ds(pl.multiple_of(at * lines, lines), lines), :
         ]
 
-    def share(level, way, step):
-        if step < 3:
-            return 0, 2 * level
-        return (0, level) if way == 0 else (level, level)
-
-    def ring_copy(level, way, step, arriving):
+    def goes(n, way, step):
+        return step < 3 or (step == 3 and way == n)
+
+    def ring_copy(level, n, way, step, arriving):
         hop = step + 1 if arriving else step
         at = ((chip - hop + chips) % chips if way == 0 else (chip + hop) % chips) * 2 + core
-        piece = strip(level, at, *share(level, way, step))
+        piece = strip(level, at, n * level, level)
         return pltpu.make_async_remote_copy(
             src_ref=piece, dst_ref=piece,
-            send_sem=ring_send.at[level - 1, way, step],
-            recv_sem=ring_recv.at[level - 1, way, step],
+            send_sem=ring_send.at[level - 1, n, way, step],
+            recv_sem=ring_recv.at[level - 1, n, way, step],
             device_id=(row, right if way == 0 else left), device_id_type=MESH,
         )
 
-    def mate_copy(level, index, arriving):
+    def mate_copy(level, n, way, step, arriving):
         whose = 1 - core if arriving else core
-        if index == 0:
-            at, part = chip, (0, 2 * level)
+        if step < 0:
+            at, index = chip, 0
         else:
-            way, step = (index - 1) // 4, (index - 1) % 4
             at = (chip - step - 1 + chips) % chips if way == 0 else (chip + step + 1) % chips
-            part = share(level, way, step)
-        piece = strip(level, at * 2 + whose, *part)
+            index = 1 + way * 4 + step
+        piece = strip(level, at * 2 + whose, n * level, level)
         return pltpu.make_async_remote_copy(
             src_ref=piece, dst_ref=piece,
-            send_sem=mate_send.at[level - 1, index],
-            recv_sem=mate_recv.at[level - 1, index],
+            send_sem=mate_send.at[level - 1, n, index],
+            recv_sem=mate_recv.at[level - 1, n, index],
             device_id=(row, mate), device_id_type=MESH,
         )
 
@@ -109,20 +134,29 @@
         lax.fori_loop(0, 2, one, 0)
 
     def ring(level, step):
+        for n in (0, 1):
+            for way in (0, 1):
+                if step > 0 and goes(n, way, step - 1):
+                    ring_copy(level, n, way, step - 1, True).wait_recv()
+                if goes(n, way, step):
+                    ring_copy(level, n, way, step, False).start()
+            for way in (0, 1):
+                if step == 0 and way == 0:
+                    mate_copy(level, n, 0, -1, False).start()
+                if step > 0 and goes(n, way, step - 1):
+                    mate_copy(level, n, way, step - 1, False).start()
+
+    def mates(n):
+        yield 0, -1
         for way in (0, 1):
-            if step > 0:
-                ring_copy(level, way, step - 1, True).wait_recv()
-            if step < 4:
-                ring_copy(level, way, step, False).start()
-        if step == 0:
-            mate_copy(level, 0, False).start()
-        else:
-            mate_copy(level, step, False).start()
-            mate_copy(level, 4 + step, False).start()
+            for step in range(4):
+                if goes(n, way, step):
+                    yield way, step
 
     def ring_end(level):
-        for index in range(9):
-            mate_copy(level, index, True).wait_recv()
+        for n in (0, 1):
+            for way, step in mates(n):
+                mate_copy(level, n, way, step, True).wait_recv()
 
     def chain_part(level, n, part, there):
         d = level
@@ -138,6 +172,20 @@
             device_id=(next_row, col), device_id_type=MESH,
         )
 
+    def scale_copy(level, n, part):
+        rows = pl.ds(0, 16 if part == 0 else 8)
+        return pltpu.make_async_remote_copy(
+            src_ref=scales[level].at[n, part, rows],
+            dst_ref=scales[level].at[n + 2, part, rows],
+            send_sem=scale_send.at[level, n, part],
+            recv_sem=scale_recv.at[level, n, part],
+            device_id=(next_row, col), device_id_type=MESH,
+        )
+
+    def pass_on(level, n, part):
+        scale_copy(level, n, part).start()
+        chain_copy(level, n, part).start()
+
     def turn_copy(level, n, k):
         there = (col + k) % cols_n
         return pltpu.make_async_remote_copy(
@@ -165,6 +213,13 @@
         high = value.astype(BF16)
         return high, (value - high.astype(F32)).astype(BF16)
 
+    lane_of = lax.broadcasted_iota(jnp.int32, (lines, 128), 1)
+    per = 128 // lines
+    sixteenth = lax.broadcasted_iota(jnp.int32, (16, 128), 0)
+
+    def wide(scale):
+        return jnp.concatenate([scale] * (width // 128), axis=1)
+
     def select_and_cross(level):
         d = level - 1
         start = level * (level - 1) // 2
@@ -175,24 +230,34 @@
             parent = parents[d, node]
             own = (parent >= row * 2) & (parent < row * 2 + 2)
             slot = jnp.where(own, 0, 2) + lax.rem(parent, 2)
+            old = scales[d][slot, 0] if d else None
+            fresh = [scales[d][slot, part, 0:8, :] if d or part == 3 else None for part in (1, 2, 3)]
             for l in range(level):
                 for m in range(level):
                     if l < d and m < d:
                         entry = l * d + m
+                        which = 3 * max(l, m) + (2 if l == m else 0 if l < m else 1)
+                        scale = old[which : which + 1, :]
                     elif l < d:
-                        entry = d * d + l
+                        entry, scale = d * d + l, fresh[0][0:1, :]
                     elif m < d:
-                        entry = d * d + d + m
+                        entry, scale = d * d + d + m, fresh[1][0:1, :]
                     else:
-                        entry = d * d + 2 * d
-                    value = cands[d][slot, entry]
+                        entry, scale = d * d + 2 * d, fresh[2][0:1, :]
+                    code = cands[d][slot, entry]
                     if level < LEVELS - 1:
-                        cands[level][n, l * level + m] = value
-                    high, low = split(value)
+                        cands[level][n, l * level + m] = code
+                    high, low = split(decode(code.astype(F32)) * wide(scale))
                     lhs[m, l * lines : (l + 1) * lines, :] = high
                     lhs[m, tall + l * lines : tall + (l + 1) * lines, :] = low
             if level < LEVELS - 1:
-                chain_copy(level, n, 0).start()
+                table = old
+                for part in (0, 1, 2):
+                    if fresh[part] is not None:
+                        line = jnp.broadcast_to(fresh[part][0:1, :], (16, 128))
+                        table = line if table is None else jnp.where(sixteenth == 3 * d + part, line, table)
+                scales[level][n, 0] = table
+                pass_on(level, n, 0)
             acc[0 : 2 * tall, :] = jnp.zeros((2 * tall, width), F32)
 
             def add(m, _):
@@ -203,45 +268,74 @@
 
             lax.fori_loop(0, level, add, 0)
             crossed = -(acc[0:tall, :] + acc[tall : 2 * tall, :])
+            scale = scale_of(crossed)
+            code = encode(crossed, scale)
             for l in range(level):
-                piece = crossed[l * lines : (l + 1) * lines, :]
-                cross_out[start + l, n] = piece
+                cross_out[start + l, n] = crossed[l * lines : (l + 1) * lines, :]
                 if level < LEVELS - 1:
-                    cands[level][n, level * level + l] = piece
+                    cands[level][n, level * level + l] = code[l * lines : (l + 1) * lines, :].astype(BF16)
             if level < LEVELS - 1:
-                chain_copy(level, n, 1).start()
-            turned = jnp.transpose(crossed, (1, 0))
+                scales[level][n, 1, 0:8, :] = jnp.broadcast_to(scale, (8, 128))
+                pass_on(level, n, 1)
+            turned = jnp.transpose(code, (1, 0)).astype(BF16)
+            slab = 0 if joint(level) else n
+            first = n * tall if joint(level) else 0
             for c in range(cols_n):
-                turn_out[level - 1][n, c, :, 0:tall] = turned[c * lines : (c + 1) * lines, :]
-
-            def send(k, _):
-                turn_copy(level, n, k).start()
-                return 0
-
-            lax.fori_loop(1, cols_n, send, 0)
-            turn_in[level - 1][n, col] = turn_out[level - 1][n, col]
-            return 0
-
-        lax.fori_loop(0, 2, one, 0)
-
-    lane_of = lax.broadcasted_iota(jnp.int32, (lines, 128), 1)
-    per = 128 // lines
+                turn_out[level - 1][slab, c, 0:lines, first : first + tall] = turned[
+                    c * lines : (c + 1) * lines, :
+                ]
+                turn_out[level - 1][slab, c, lines : lines + 16, first : first + tall] = (
+                    jnp.broadcast_to(scale, (16, tall)).astype(BF16)
+                )
+            if not joint(level):
+                send_turn(level, n)
+            return 0
+
+        if joint(level):
+            one(0, 0)
+            one(1, 0)
+            send_turn(level, 0)
+        else:
+            lax.fori_loop(0, 2, one, 0)
+
+    def send_turn(level, slab):
+        def send(k, _):
+            turn_copy(level, slab, k).start()
+            return 0
+
+        lax.fori_loop(1, cols_n, send, 0)
+        turn_in[level - 1][slab, col] = turn_out[level - 1][slab, col]
+
+    def open_turn(level, slab):
+        def arrive(k, _):
+            turn_arrival(level, slab, k).wait_recv()
+            return 0
+
+        lax.fori_loop(1, cols_n, arrive, 0)
+
+        lanes = lanes_of(level)
+
+        def undo(c, _):
+            code = turn_in[level - 1][slab, c, 0:lines, :].astype(F32)
+            scale = turn_in[level - 1][slab, c, lines : lines + 16, :].astype(F32)
+            opened[c, :, 0:lanes] = decode(code) * jnp.concatenate([scale] * (lines // 16), axis=0)
+            return 0
+
+        lax.fori_loop(0, cols_n, undo, 0)
 
     def finish_level(level):
         def one(n, _):
-            def arrive(k, _):
-                turn_arrival(level, n, k).wait_recv()
-                return 0
-
-            lax.fori_loop(1, cols_n, arrive, 0)
+            if not joint(level):
+                open_turn(level, n)
             for l in range(level):
+                group = l + n * level if joint(level) else l
                 for q in range(width // 128):
                     piece = None
                     for k in range(per):
-                        source = turn_in[level - 1][
-                            n, q * per + k, :, (l // per) * 128 : (l // per) * 128 + 128
+                        source = opened[
+                            q * per + k, :, (group // per) * 128 : (group // per) * 128 + 128
                         ]
-                        shift = ((k - l % per) * lines) % 128
+                        shift = ((k - group % per) * lines) % 128
                         if shift:
                             source = pltpu.roll(source, shift, 1)
                         piece = source if piece is None else jnp.where(lane_of >= k * lines, source, piece)
@@ -249,9 +343,15 @@
                     lhs[l, 0:lines, q * 128 : (q + 1) * 128] = high
                     lhs[l, lines : 2 * lines, q * 128 : (q + 1) * 128] = low
                     if level < LEVELS - 1:
-                        cands[level][n, level * level + level + l, :, q * 128 : (q + 1) * 128] = piece
+                        turned_f32[l * lines : (l + 1) * lines, q * 128 : (q + 1) * 128] = piece
             if level < LEVELS - 1:
-                chain_copy(level, n, 2).start()
+                whole = turned_f32[0 : level * lines, :]
+                scale = scale_of(whole)
+                code = encode(whole, scale).astype(BF16)
+                for l in range(level):
+                    cands[level][n, level * level + level + l] = code[l * lines : (l + 1) * lines, :]
+                scales[level][n, 2, 0:8, :] = jnp.broadcast_to(scale, (8, 128))
+                pass_on(level, n, 2)
             acc[0 : 2 * lines, :] = jnp.zeros((2 * lines, width), F32)
 
             def add(l, _):
@@ -264,19 +364,28 @@
             marginal = base_of(level, n) - (acc[0:lines, :] + acc[lines : 2 * lines, :])
             marg_out[level, n] = marginal
             if level < LEVELS - 1:
-                cands[level][n, level * level + 2 * level] = marginal
-                chain_copy(level, n, 3).start()
-            return 0
-
-        lax.fori_loop(0, 2, one, 0)
+                send_marginal(level, n, marginal)
+            return 0
+
+        if joint(level):
+            open_turn(level, 0)
+            one(0, 0)
+            one(1, 0)
+        else:
+            lax.fori_loop(0, 2, one, 0)
+
+    def send_marginal(level, n, marginal):
+        scale = scale_of(marginal)
+        cands[level][n, level * level + 2 * level] = encode(marginal, scale).astype(BF16)
+        scales[level][n, 3, 0:8, :] = jnp.broadcast_to(scale, (8, 128))
+        pass_on(level, n, 3)
 
     mask_factor(1)
     ring(1, 0)
     for n in range(2):
         marginal = base_of(0, n)
         marg_out[0, n] = marginal
-        cands[0][n, 0] = marginal
-        chain_copy(0, n, 3).start()
+        send_marginal(0, n, marginal)
     mask_factor(2)
     ring(2, 0)
     ring(1, 1)
@@ -290,15 +399,16 @@
     ring(2, 3)
     ring(3, 0)
     ring(1, 4)
-    before = {1: (), 2: ((2, 4),), 3: ((3, 4),), 4: ((4, 4),), 5: ((5, 4),)}
-    middle = {1: ((3, 1), (3, 2)), 2: ((4, 0), (4, 1)), 3: ((5, 1), (5, 2)), 4: (), 5: ()}
-    after = {1: ((3, 3),), 2: ((4, 2), (4, 3), (5, 0)), 3: ((5, 3),), 4: (), 5: ()}
+    before = {1: (), 2: ((3, 3), (4, 0)), 3: ((4, 2),), 4: ((4, 4), (5, 1)), 5: ((5, 4),)}
+    middle = {1: ((2, 4), (3, 1)), 2: ((3, 4), (4, 1)), 3: ((4, 3), (5, 0)), 4: ((5, 2), (5, 3)), 5: ()}
+    after = {1: ((3, 2),), 2: (), 3: (), 4: (), 5: ()}
     for level in range(1, LEVELS):
         for job in before[level]:
             ring(*job)
         ring_end(level)
         for n in range(2):
             for part in parts_of(level - 1):
+                scale_copy(level - 1, n, part).wait_recv()
                 chain_copy(level - 1, n, part).wait_recv()
         select_and_cross(level)
         for job in middle[level]:
@@ -308,21 +418,25 @@
             ring(*job)
 
     for level in range(1, LEVELS):
-        for way in (0, 1):
-            for step in range(4):
-                ring_copy(level, way, step, False).wait_send()
-        for index in range(9):
-            mate_copy(level, index, False).wait_send()
+        for n in (0, 1):
+            for way in (0, 1):
+                for step in range(4):
+                    if goes(n, way, step):
+                        ring_copy(level, n, way, step, False).wait_send()
+            for way, step in mates(n):
+                mate_copy(level, n, way, step, False).wait_send()
 
         def sent(k, _):
             turn_copy(level, 0, k).wait_send()
-            turn_copy(level, 1, k).wait_send()
+            if not joint(level):
+                turn_copy(level, 1, k).wait_send()
             return 0
 
         lax.fori_loop(1, cols_n, sent, 0)
     for level in range(LEVELS - 1):
         for n in range(2):
             for part in parts_of(level):
+                scale_copy(level, n, part).wait_send()
                 chain_copy(level, n, part).wait_send()
 
 
@@ -334,6 +448,10 @@
         vmem = pl.BlockSpec(memory_space=pltpu.VMEM)
         smem = pl.BlockSpec(memory_space=pltpu.SMEM)
         dma = pltpu.SemaphoreType.DMA
+
+        def turn_shape(level):
+            return (1 if joint(level) else 2, cols_n, lines + 16, lanes_of(level))
+
         return pl.pallas_call(
             functools.partial(kernel, rows_n, cols_n),
             out_shape=(
@@ -343,16 +461,21 @@
             in_specs=[vmem, vmem, smem, smem],
             out_specs=(vmem, vmem),
             scratch_shapes=[
-                *[pltpu.VMEM((4, (d + 1) * (d + 1), lines, width), F32) for d in range(5)],
+                *[pltpu.VMEM((4, (d + 1) * (d + 1), lines, width), BF16) for d in range(5)],
                 *[pltpu.VMEM((2 * d, width, width), BF16) for d in range(1, 6)],
-                *[pltpu.VMEM((2, cols_n, lines, lanes_of(d)), F32) for d in range(1, 6)],
-                *[pltpu.VMEM((2, cols_n, lines, lanes_of(d)), F32) for d in range(1, 6)],
+                *[pltpu.VMEM(turn_shape(d), BF16) for d in range(1, 6)],
+                *[pltpu.VMEM(turn_shape(d), BF16) for d in range(1, 6)],
+                *[pltpu.VMEM((4, 4, 16, 128), F32) for d in range(5)],
                 pltpu.VMEM((5, 320, width), BF16),
                 pltpu.VMEM((320, width), F32),
+                pltpu.VMEM((cols_n, lines, 256), F32),
+                pltpu.VMEM((4 * lines, width), F32),
+                dma((5, 2, 2, 4)),
+                dma((5, 2, 2, 4)),
+                dma((5, 2, 9)),
+                dma((5, 2, 9)),
                 dma((5, 2, 4)),
                 dma((5, 2, 4)),
-                dma((5, 9)),
-                dma((5, 9)),
                 dma((5, 2, 4)),
                 dma((5, 2, 4)),
                 dma((5, 2, cols_n)),

time: 255 us -> 172 us (0.67)
  Pallas kernels: 250 us -> 167 us
    pallas_call x1, Pallas kernels: 250 us -> 167 us  [shards(): pl.pallas_call(functools.partial(kernel, rows_n, cols_n), out_shape=(jax....]
where the time goes in v2:
time: 172 us; the launch traced here: 171 us
  Pallas kernels  167 us (97%)
  local copies, waits for them, and re-layouts  4.03 us (2%)
    pallas_call x1, Pallas kernels, shards(): pl.pallas_call(functools.partial(kernel, rows_n, cols_n), out_shape=(jax....  167 us
    unnamed x4, local copies, waits for them, and re-layouts  4.03 us

profile of v2, /device:TPU:1, one launch (start us, length us, event | category | flops | bytes accessed | tf_op | source)
XLA Modules:
  0.0 171.5 jit_solution(12836788216790956333)
XLA Ops:
  0.6 166.8 %shard_map.59 = (f32[15,2,32,512]{3,2,1,0:T(8,128)}, f32[6,2,32,512]{3,2,1,0:T(8,128)}) custom-call(bf16[15,2,32,512]{3,2,1,0:T(8,128)(2,1)} %panel.1, f32[6,2,32,512]{3,2,1,0:T(8,128)} %diag.1, s32[5,32]{1,0:T(8,128)} %parents.1, s32[6,32]{1,0:T(8,128)} %sizes.1), custom_call_target="tpu_custom_call" | custom-call | tf_op jit(solution)/shard_map/pallas_call | solution.py:455
  167.4 0.0 copy-start
  167.4 3.1 %copy.8 = f32[15,2,32,512]{3,2,1,0:T(8,128)} copy(f32[15,2,32,512]{3,2,1,0:T(8,128)} %get-tuple-element.4) | data formatting | bytes 3932160
  170.6 0.0 copy-done
  170.6 0.9 copy.9
Async XLA Ops:
  167.4 3.2 %copy-start = (f32[6,2,32,512]{3,2,1,0:T(8,128)S(1)}, f32[6,2,32,512]{3,2,1,0:T(8,128)}, u32[]{:S(2)}) copy-start(f32[6,2,32,512]{3,2,1,0:T(8,128)} %get-tuple-element.5) | copy-start | bytes 2359300

commit v3 on v2

v3 whole, which is shorter than its diff:
```python
import functools

import jax
import jax.numpy as jnp
from jax import lax
from jax.experimental import pallas as pl
from jax.experimental.pallas import tpu as pltpu
from jax.sharding import PartitionSpec as P

MESH = pl.DeviceIdType.MESH
LEVELS = 6
F32 = jnp.float32
BF16 = jnp.bfloat16


POWER = 6
PREPARE = ((2, 0), (1, 1), (2, 1), (1, 2), (2, 2), (1, 3), (2, 3), (3, 0), (1, 4))
BEFORE = {1: (), 2: ((3, 3), (4, 0)), 3: ((4, 2),), 4: ((4, 4), (5, 1)), 5: ((5, 4),)}
MIDDLE = {1: ((2, 4), (3, 1)), 2: ((3, 4), (4, 1)), 3: ((4, 3), (5, 0)), 4: ((5, 2), (5, 3)), 5: ()}
AFTER = {1: ((3, 2),), 2: (), 3: (), 4: (), 5: ()}


def joint(level):
    return level <= 2


def lanes_of(level):
    tall = 32 * level * (2 if joint(level) else 1)
    return 128 * (-(-tall // 128))


def scale_of(value):
    top = jnp.max(jnp.max(jnp.abs(value), axis=0, keepdims=True), axis=1, keepdims=True)
    return jnp.maximum(top, 1e-30).astype(BF16).astype(F32)


def encode(value, scale):
    unit = value * (1.0 / scale)
    square = unit * unit
    return unit * jnp.abs(unit) * (square * square)


def decode(code):
    root = jnp.exp(jnp.log(jnp.abs(code)) * (1.0 / POWER))
    return jnp.where(code > 0.0, root, jnp.where(code < 0.0, -root, 0.0))


def kernel(rows_n, cols_n, panel, diag, parents, sizes, cross_out, marg_out, *scratch):
    cands = scratch[0:5]
    fulls = scratch[5:10]
    turn_out = scratch[10:15]
    turn_in = scratch[15:20]
    scales = scratch[20:25]
    (
        lhs, acc, opened, turned_f32, mark_out, mark_in, factor_send, ring_recv, mate_recv,
        chain_send, chain_recv, scale_send, scale_recv, turn_send, turn_recv, mark_send, mark_recv,
    ) = scratch[25:]
    width = diag.shape[3]
    lines = diag.shape[2]
    chips = cols_n // 2
    row = lax.axis_index("row")
    col = lax.axis_index("col")
    chip = col // 2
    core = col % 2
    mate = col + 1 - 2 * core
    right = (col + 2) % cols_n
    left = (col + cols_n - 2) % cols_n
    next_row = (row + 1) % rows_n
    prev_row = (row + rows_n - 1) % rows_n

    barrier = pltpu.get_barrier_semaphore()
    for k in range(1, cols_n):
        pl.semaphore_signal(barrier, inc=1, device_id=(row, (col + k) % cols_n), device_id_type=MESH)
    pl.semaphore_signal(barrier, inc=1, device_id=(next_row, col), device_id_type=MESH)
    pl.semaphore_signal(barrier, inc=1, device_id=(prev_row, col), device_id_type=MESH)
    line_of = lax.broadcasted_iota(jnp.int32, (lines, width), 0) + col * lines
    column_of = lax.broadcasted_iota(jnp.int32, (lines, width), 1)

    def base_of(level, n):
        size = sizes[level, row * 2 + n]
        live = (line_of < size) & (column_of < size)
        eye = (line_of == column_of) & (line_of >= size)
        return jnp.where(live, diag[level, n], jnp.where(eye, 1.0, 0.0))

    def strip(level, at, first, count):
        return fulls[level - 1].at[
            pl.ds(first, count), pl.ds(pl.multiple_of(at * lines, lines), lines), :
        ]

    def goes(n, way, step):
        return step < 3 or (step == 3 and way == n)

    def ring_copy(level, n, way, step):
        at = ((chip - step + chips) % chips if way == 0 else (chip + step) % chips) * 2 + core
        piece = strip(level, at, n * level, level)
        return pltpu.make_async_remote_copy(
            src_ref=piece, dst_ref=piece,
            send_sem=factor_send.at[level - 1],
            recv_sem=ring_recv.at[level - 1, n, step],
            device_id=(row, right if way == 0 else left), device_id_type=MESH,
        )

    def mate_copy(level, n, way, step):
        if step < 0:
            at = chip
        else:
            at = (chip - step - 1 + chips) % chips if way == 0 else (chip + step + 1) % chips
        piece = strip(level, at * 2 + core, n * level, level)
        return pltpu.make_async_remote_copy(
            src_ref=piece, dst_ref=piece,
            send_sem=factor_send.at[level - 1],
            recv_sem=mate_recv.at[level - 1, n],
            device_id=(row, mate), device_id_type=MESH,
        )

    def factor_wait(level, first, count, strips, send, recv):
        piece = fulls[level - 1].at[pl.ds(first, count), pl.ds(0, strips * lines), :]
        return pltpu.make_async_remote_copy(
            src_ref=piece, dst_ref=piece, send_sem=send, recv_sem=recv,
            device_id=(row, mate), device_id_type=MESH,
        )

    def mask_factor(level):
        start = level * (level - 1) // 2

        def one(n, _):
            node = row * 2 + n
            size = sizes[level, node]
            above = node
            for up in range(level - 1, -1, -1):
                above = parents[up, above]
                upper = sizes[up, above]
                keep = (line_of < upper) & (column_of < size)
                block = jnp.where(keep, panel[start + up, n].astype(F32), 0.0)
                fulls[level - 1][
                    n * level + up, pl.ds(pl.multiple_of(col * lines, lines), lines), :
                ] = block.astype(BF16)
            return 0

        lax.fori_loop(0, 2, one, 0)

    def ring(level, step):
        for n in (0, 1):
            came = [way for way in (0, 1) if step > 0 and goes(n, way, step - 1)]
            if came:
                factor_wait(
                    level, n * level, level, len(came), factor_send.at[level - 1], ring_recv.at[level - 1, n, step - 1]
                ).wait_recv()
            for way in (0, 1):
                if goes(n, way, step):
                    ring_copy(level, n, way, step).start()
            if step == 0:
                mate_copy(level, n, 0, -1).start()
            for way in came:
                mate_copy(level, n, way, step - 1).start()

    def ring_end(level):
        for n in (0, 1):
            factor_wait(
                level, n * level, level, 8, factor_send.at[level - 1], mate_recv.at[level - 1, n]
            ).wait_recv()

    def ring_sent(level):
        factor_wait(
            level, 0, 2 * level, 15, factor_send.at[level - 1], mate_recv.at[level - 1, 0]
        ).wait_send()

    def chain_part(level, n, part, there):
        d = level
        first, count = ((0, d * d), (d * d, d), (d * d + d, d), (d * d + 2 * d, 1))[part]
        return cands[d].at[n + 2 if there else n, pl.ds(first, count)]

    def remote(src, dst, send, recv, place):
        return pltpu.make_async_remote_copy(
            src_ref=src, dst_ref=dst, send_sem=send, recv_sem=recv, device_id=place, device_id_type=MESH
        )

    def scale_part(level, n, part):
        first, count = (0, 3 * level) if part == 0 else (3 * level + part - 1, 1)
        if level == 0:
            first, count = 0, 3
        return scales[level].at[n, pl.ds(first, count)]

    def pass_on(level, n, part):
        place = (next_row, col)
        remote(
            scale_part(level, n, part), scale_part(level, n + 2, part),
            scale_send.at[level], scale_recv.at[level], place,
        ).start()
        remote(
            chain_part(level, n, part, False), chain_part(level, n, part, True),
            chain_send.at[level], chain_recv.at[level], place,
        ).start()

    def chain_all(level):
        ours, theirs, place = pl.ds(0, 2), pl.ds(2, 2), (next_row, col)
        return (
            remote(scales[level].at[ours], scales[level].at[theirs], scale_send.at[level], scale_recv.at[level], place),
            remote(cands[level].at[ours], cands[level].at[theirs], chain_send.at[level], chain_recv.at[level], place),
        )

    def turn_copies(level, slab, k):
        there = (col + k) % cols_n
        place = (row, there)
        return (
            remote(
                mark_out.at[level - 1, slab], mark_in.at[level - 1, slab, col],
                mark_send.at[level - 1, slab], mark_recv.at[level - 1, slab], place,
            ),
            remote(
                turn_out[level - 1].at[slab, there], turn_in[level - 1].at[slab, col],
                turn_send.at[level - 1, slab], turn_recv.at[level - 1, slab], place,
            ),
        )

    def turn_all(level, slab):
        most, place = pl.ds(0, cols_n - 1), (row, mate)
        marks = mark_in.at[level - 1, slab, most]
        pieces = turn_in[level - 1].at[slab, most]
        return (
            remote(marks, marks, mark_send.at[level - 1, slab], mark_recv.at[level - 1, slab], place),
            remote(pieces, pieces, turn_send.at[level - 1, slab], turn_recv.at[level - 1, slab], place),
        )

    def parts_of(level):
        return (3,) if level == 0 else (0, 1, 2, 3)

    def split(value):
        high = value.astype(BF16)
        return high, (value - high.astype(F32)).astype(BF16)

    lane_of = lax.broadcasted_iota(jnp.int32, (lines, 128), 1)
    per = 128 // lines
    sixteenth = lax.broadcasted_iota(jnp.int32, (16, 128), 0)

    def wide(scale):
        return jnp.concatenate([scale] * (width // 128), axis=1)

    def select_and_cross(level):
        d = level - 1
        start = level * (level - 1) // 2
        tall = lines * level

        def one(n, _):
            node = row * 2 + n
            parent = parents[d, node]
            own = (parent >= row * 2) & (parent < row * 2 + 2)
            slot = jnp.where(own, 0, 2) + lax.rem(parent, 2)
            table = scales[d][slot]
            if level < LEVELS - 1:
                scales[level][n, 0 : 3 * level] = table
            for l in range(level):
                for m in range(level):
                    if l < d and m < d:
                        entry = l * d + m
                    elif l < d:
                        entry = d * d + l
                    elif m < d:
                        entry = d * d + d + m
                    else:
                        entry = d * d + 2 * d
                    scale = table[3 * max(l, m) + (2 if l == m else 0 if l < m else 1)]
                    code = cands[d][slot, entry]
                    if level < LEVELS - 1:
                        cands[level][n, l * level + m] = code
                    high, low = split(decode(code.astype(F32)) * wide(scale))
                    lhs[m, l * lines : (l + 1) * lines, :] = high
                    lhs[m, tall + l * lines : tall + (l + 1) * lines, :] = low
            if level < LEVELS - 1:
                pass_on(level, n, 0)
            acc[0 : 2 * tall, :] = jnp.zeros((2 * tall, width), F32)

            def add(m, _):
                acc[0 : 2 * tall, :] += jnp.dot(
                    lhs[m, 0 : 2 * tall, :], fulls[level - 1][n * level + m], preferred_element_type=F32
                )
                return 0

            lax.fori_loop(0, level, add, 0)
            crossed = -(acc[0:tall, :] + acc[tall : 2 * tall, :])
            scale = scale_of(crossed)
            code = encode(crossed, scale)
            for l in range(level):
                cross_out[start + l, n] = crossed[l * lines : (l + 1) * lines, :]
                if level < LEVELS - 1:
                    cands[level][n, level * level + l] = code[l * lines : (l + 1) * lines, :].astype(BF16)
            if level < LEVELS - 1:
                scales[level][n, 3 * level] = jnp.broadcast_to(scale, (1, 128))
                pass_on(level, n, 1)
            turned = jnp.transpose(code, (1, 0)).astype(BF16)
            slab = 0 if joint(level) else n
            first = n * tall if joint(level) else 0
            for c in range(cols_n):
                turn_out[level - 1][slab, c, :, first : first + tall] = turned[
                    c * lines : (c + 1) * lines, :
                ]
            lane = lax.broadcasted_iota(jnp.int32, (1, 128), 1)
            mark = jnp.broadcast_to(scale, (1, 128))
            if joint(level) and n == 1:
                mark = jnp.where(lane < tall, mark_out[level - 1, 0], mark)
            mark_out[level - 1, slab] = mark
            if not joint(level):
                send_turn(level, n)
            return 0

        if joint(level):
            one(0, 0)
            one(1, 0)
            send_turn(level, 0)
        else:
            lax.fori_loop(0, 2, one, 0)

    def send_turn(level, slab):
        def send(k, _):
            for copy in turn_copies(level, slab, k):
                copy.start()
            return 0

        lax.fori_loop(1, cols_n, send, 0)
        turn_in[level - 1][slab, col] = turn_out[level - 1][slab, col]
        mark_in[level - 1, slab, col] = mark_out[level - 1, slab]

    def open_turn(level, slab):
        for copy in turn_all(level, slab):
            copy.wait_recv()
        lanes = lanes_of(level)

        def undo(c, _):
            code = turn_in[level - 1][slab, c].astype(F32)
            mark = jnp.concatenate([mark_in[level - 1, slab, c]] * (lanes // 128), axis=1)
            opened[c, :, 0:lanes] = decode(code) * mark
            return 0

        lax.fori_loop(0, cols_n, undo, 0)

    def finish_level(level):
        def one(n, _):
            if not joint(level):
                open_turn(level, n)
            for l in range(level):
                group = l + n * level if joint(level) else l
                for q in range(width // 128):
                    piece = None
                    for k in range(per):
                        source = opened[
                            q * per + k, :, (group // per) * 128 : (group // per) * 128 + 128
                        ]
                        shift = ((k - group % per) * lines) % 128
                        if shift:
                            source = pltpu.roll(source, shift, 1)
                        piece = source if piece is None else jnp.where(lane_of >= k * lines, source, piece)
                    high, low = split(piece)
                    lhs[l, 0:lines, q * 128 : (q + 1) * 128] = high
                    lhs[l, lines : 2 * lines, q * 128 : (q + 1) * 128] = low
                    if level < LEVELS - 1:
                        turned_f32[l * lines : (l + 1) * lines, q * 128 : (q + 1) * 128] = piece
            if level < LEVELS - 1:
                whole = turned_f32[0 : level * lines, :]
                scale = scale_of(whole)
                code = encode(whole, scale).astype(BF16)
                for l in range(level):
                    cands[level][n, level * level + level + l] = code[l * lines : (l + 1) * lines, :]
                scales[level][n, 3 * level + 1] = jnp.broadcast_to(scale, (1, 128))
                pass_on(level, n, 2)
            acc[0 : 2 * lines, :] = jnp.zeros((2 * lines, width), F32)

            def add(l, _):
                acc[0 : 2 * lines, :] += jnp.dot(
                    lhs[l, 0 : 2 * lines, :], fulls[level - 1][n * level + l], preferred_element_type=F32
                )
                return 0

            lax.fori_loop(0, level, add, 0)
            marginal = base_of(level, n) - (acc[0:lines, :] + acc[lines : 2 * lines, :])
            marg_out[level, n] = marginal
            if level < LEVELS - 1:
                send_marginal(level, n, marginal)
            return 0

        if joint(level):
            open_turn(level, 0)
            one(0, 0)
            one(1, 0)
        else:
            lax.fori_loop(0, 2, one, 0)

    def keep_marginal(level, n, marginal):
        scale = scale_of(marginal)
        cands[level][n, level * level + 2 * level] = encode(marginal, scale).astype(BF16)
        for entry in range(3) if level == 0 else (3 * level + 2,):
            scales[level][n, entry] = jnp.broadcast_to(scale, (1, 128))

    def send_marginal(level, n, marginal):
        keep_marginal(level, n, marginal)
        pass_on(level, n, 3)

    mask_factor(1)
    for n in range(2):
        marginal = base_of(0, n)
        marg_out[0, n] = marginal
        keep_marginal(0, n, marginal)
    for level in range(2, LEVELS):
        mask_factor(level)
    pl.semaphore_wait(barrier, cols_n + 1)
    ring(1, 0)
    pass_on(0, 0, 3)
    pass_on(0, 1, 3)
    for job in PREPARE:
        ring(*job)
    for level in range(1, LEVELS):
        for job in BEFORE[level]:
            ring(*job)
        ring_end(level)
        for copy in chain_all(level - 1):
            copy.wait_recv()
        select_and_cross(level)
        for job in MIDDLE[level]:
            ring(*job)
        finish_level(level)
        for job in AFTER[level]:
            ring(*job)

    for level in range(1, LEVELS):
        ring_sent(level)
        for slab in (0,) if joint(level) else (0, 1):
            for copy in turn_all(level, slab):
                copy.wait_send()
        for copy in chain_all(level - 1):
            copy.wait_send()


def solution(mesh):
    rows_n, cols_n = mesh.shape["row"], mesh.shape["col"]

    def shards(panel, diag_inverse, parents, sizes):
        pairs, per, lines, width = panel.shape
        vmem = pl.BlockSpec(memory_space=pltpu.VMEM)
        smem = pl.BlockSpec(memory_space=pltpu.SMEM)
        dma = pltpu.SemaphoreType.DMA

        def turn_shape(level):
            return (1 if joint(level) else 2, cols_n, lines, lanes_of(level))

        return pl.pallas_call(
            functools.partial(kernel, rows_n, cols_n),
            out_shape=(
                jax.ShapeDtypeStruct((pairs, per, lines, width), F32),
                jax.ShapeDtypeStruct((LEVELS, per, lines, width), F32),
            ),
            in_specs=[vmem, vmem, smem, smem],
            out_specs=(vmem, vmem),
            scratch_shapes=[
                *[pltpu.VMEM((4, (d + 1) * (d + 1), lines, width), BF16) for d in range(5)],
                *[pltpu.VMEM((2 * d, width, width), BF16) for d in range(1, 6)],
                *[pltpu.VMEM(turn_shape(d), BF16) for d in range(1, 6)],
                *[pltpu.VMEM(turn_shape(d), BF16) for d in range(1, 6)],
                *[pltpu.VMEM((4, 3 * (d + 1), 1, 128), F32) for d in range(5)],
                pltpu.VMEM((5, 320, width), BF16),
                pltpu.VMEM((320, width), F32),
                pltpu.VMEM((cols_n, lines, 256), F32),
                pltpu.VMEM((4 * lines, width), F32),
                pltpu.VMEM((5, 2, 1, 128), F32),
                pltpu.VMEM((5, 2, cols_n, 1, 128), F32),
                dma((5,)),
                dma((5, 2, 4)),
                dma((5, 2)),
                dma((5,)),
                dma((5,)),
                dma((5,)),
                dma((5,)),
                dma((5, 2)),
                dma((5, 2)),
                dma((5, 2)),
                dma((5, 2)),
            ],
            compiler_params=pltpu.CompilerParams(
                collective_id=0, has_side_effects=True, vmem_limit_bytes=64000 * 1024
            ),
        )(panel, diag_inverse, parents, sizes)

    in_specs = (P(None, "row", "col", None), P(None, "row", "col", None), P(), P())
    out_specs = (P(None, "row", "col", None), P(None, "row", "col", None))
    return jax.shard_map(shards, mesh=mesh, in_specs=in_specs, out_specs=out_specs, check_vma=False)
```

time: 172 us -> 155 us (0.901)
  Pallas kernels: 167 us -> 150 us
    pallas_call x1, Pallas kernels: 167 us -> 150 us  [shards(): pl.pallas_call(functools.partial(kernel, rows_n, cols_n), out_shape=(jax....]
where the time goes in v3:
time: 155 us
  Pallas kernels  150 us (97%)
  local copies, waits for them, and re-layouts  4.03 us (3%)
    pallas_call x1, Pallas kernels, shards(): pl.pallas_call(functools.partial(kernel, rows_n, cols_n), out_shape=(jax....  150 us
    unnamed x4, local copies, waits for them, and re-layouts  4.03 us

profile of v3, /device:TPU:1, one launch (start us, length us, event | category | flops | bytes accessed | tf_op | source)
XLA Modules:
  0.0 154.9 jit_solution(16892635257737466600)
XLA Ops:
  0.6 150.2 %shard_map.59 = (f32[15,2,32,512]{3,2,1,0:T(8,128)}, f32[6,2,32,512]{3,2,1,0:T(8,128)}) custom-call(bf16[15,2,32,512]{3,2,1,0:T(8,128)(2,1)} %panel.1, f32[6,2,32,512]{3,2,1,0:T(8,128)} %diag.1, s32[5,32]{1,0:T(8,128)} %parents.1, s32[6,32]{1,0:T(8,128)} %sizes.1), custom_call_target="tpu_custom_call" | custom-call | tf_op jit(solution)/shard_map/pallas_call | solution.py:444
  150.9 0.0 copy-start
  150.9 3.1 %copy.8 = f32[15,2,32,512]{3,2,1,0:T(8,128)} copy(f32[15,2,32,512]{3,2,1,0:T(8,128)} %get-tuple-element.4) | data formatting | bytes 3932160
  154.0 0.0 copy-done
  154.0 0.9 copy.9
Async XLA Ops:
  150.9 3.2 %copy-start = (f32[6,2,32,512]{3,2,1,0:T(8,128)S(1)}, f32[6,2,32,512]{3,2,1,0:T(8,128)}, u32[]{:S(2)}) copy-start(f32[6,2,32,512]{3,2,1,0:T(8,128)} %get-tuple-element.5) | copy-start | bytes 2359300

commit v4 on v3

--- a/solution.py
+++ b/solution.py
@@ -52,7 +52,7 @@
     turn_in = scratch[15:20]
     scales = scratch[20:25]
     (
-        lhs, acc, opened, turned_f32, mark_out, mark_in, factor_send, ring_recv, mate_recv,
+        lhs, opened, turned_f32, mark_out, mark_in, factor_send, ring_recv, mate_recv,
         chain_send, chain_recv, scale_send, scale_recv, turn_send, turn_recv, mark_send, mark_recv,
     ) = scratch[25:]
     width = diag.shape[3]
@@ -264,20 +264,16 @@
                     if level < LEVELS - 1:
                         cands[level][n, l * level + m] = code
                     high, low = split(decode(code.astype(F32)) * wide(scale))
-                    lhs[m, l * lines : (l + 1) * lines, :] = high
-                    lhs[m, tall + l * lines : tall + (l + 1) * lines, :] = low
+                    lhs[l * lines : (l + 1) * lines, m * width : (m + 1) * width] = high
+                    lhs[tall + l * lines : tall + (l + 1) * lines, m * width : (m + 1) * width] = low
             if level < LEVELS - 1:
                 pass_on(level, n, 0)
-            acc[0 : 2 * tall, :] = jnp.zeros((2 * tall, width), F32)
-
-            def add(m, _):
-                acc[0 : 2 * tall, :] += jnp.dot(
-                    lhs[m, 0 : 2 * tall, :], fulls[level - 1][n * level + m], preferred_element_type=F32
-                )
-                return 0
-
-            lax.fori_loop(0, level, add, 0)
-            crossed = -(acc[0:tall, :] + acc[tall : 2 * tall, :])
+            both = jnp.dot(
+                lhs[0 : 2 * tall, 0 : level * width],
+                fulls[level - 1][pl.ds(n * level, level)].reshape(level * width, width),
+                preferred_element_type=F32,
+            )
+            crossed = -(both[0:tall, :] + both[tall : 2 * tall, :])
             scale = scale_of(crossed)
             code = encode(crossed, scale)
             for l in range(level):
@@ -350,8 +346,8 @@
                             source = pltpu.roll(source, shift, 1)
                         piece = source if piece is None else jnp.where(lane_of >= k * lines, source, piece)
                     high, low = split(piece)
-                    lhs[l, 0:lines, q * 128 : (q + 1) * 128] = high
-                    lhs[l, lines : 2 * lines, q * 128 : (q + 1) * 128] = low
+                    lhs[0:lines, l * width + q * 128 : l * width + (q + 1) * 128] = high
+                    lhs[lines : 2 * lines, l * width + q * 128 : l * width + (q + 1) * 128] = low
                     if level < LEVELS - 1:
                         turned_f32[l * lines : (l + 1) * lines, q * 128 : (q + 1) * 128] = piece
             if level < LEVELS - 1:
@@ -362,16 +358,12 @@
                     cands[level][n, level * level + level + l] = code[l * lines : (l + 1) * lines, :]
                 scales[level][n, 3 * level + 1] = jnp.broadcast_to(scale, (1, 128))
                 pass_on(level, n, 2)
-            acc[0 : 2 * lines, :] = jnp.zeros((2 * lines, width), F32)
-
-            def add(l, _):
-                acc[0 : 2 * lines, :] += jnp.dot(
-                    lhs[l, 0 : 2 * lines, :], fulls[level - 1][n * level + l], preferred_element_type=F32
-                )
-                return 0
-
-            lax.fori_loop(0, level, add, 0)
-            marginal = base_of(level, n) - (acc[0:lines, :] + acc[lines : 2 * lines, :])
+            both = jnp.dot(
+                lhs[0 : 2 * lines, 0 : level * width],
+                fulls[level - 1][pl.ds(n * level, level)].reshape(level * width, width),
+                preferred_element_type=F32,
+            )
+            marginal = base_of(level, n) - (both[0:lines, :] + both[lines : 2 * lines, :])
             marg_out[level, n] = marginal
             if level < LEVELS - 1:
                 send_marginal(level, n, marginal)
@@ -455,8 +447,7 @@
                 *[pltpu.VMEM(turn_shape(d), BF16) for d in range(1, 6)],
                 *[pltpu.VMEM(turn_shape(d), BF16) for d in range(1, 6)],
                 *[pltpu.VMEM((4, 3 * (d + 1), 1, 128), F32) for d in range(5)],
-                pltpu.VMEM((5, 320, width), BF16),
-                pltpu.VMEM((320, width), F32),
+                pltpu.VMEM((320, 5 * width), BF16),
                 pltpu.VMEM((cols_n, lines, 256), F32),
                 pltpu.VMEM((4 * lines, width), F32),
                 pltpu.VMEM((5, 2, 1, 128), F32),
@@ -474,7 +465,7 @@
                 dma((5, 2)),
             ],
             compiler_params=pltpu.CompilerParams(
-                collective_id=0, has_side_effects=True, vmem_limit_bytes=64000 * 1024
+                collective_id=0, has_side_effects=True, vmem_limit_bytes=44000 * 1024
             ),
         )(panel, diag_inverse, parents, sizes)
 

time: 155 us -> 153 us (0.987)
  Pallas kernels: 150 us -> 146 us
  local copies, waits for them, and re-layouts: 4.03 us -> 5.85 us
    pallas_call x1, Pallas kernels: 150 us -> 146 us  [shards(): pl.pallas_call(functools.partial(kernel, rows_n, cols_n), out_shape=(jax....]
    unnamed x4 -> x10, local copies, waits for them, and re-layouts: 4.03 us -> 5.85 us
where the time goes in v4:
time: 153 us
  Pallas kernels  146 us (95%)
  local copies, waits for them, and re-layouts  5.85 us (4%)
    pallas_call x1, Pallas kernels, shards(): pl.pallas_call(functools.partial(kernel, rows_n, cols_n), out_shape=(jax....  146 us
    unnamed x10, local copies, waits for them, and re-layouts  5.85 us

profile of v4, /device:TPU:1, one launch (start us, length us, event | category | flops | bytes accessed | tf_op | source)
XLA Modules:
  0.0 152.9 jit_solution(7818727266337728440)
XLA Ops:
  0.6 0.0 copy-start
  0.6 1.2 copy-done
  1.8 0.0 copy-start.1
  1.8 1.1 copy-done.1
  3.0 0.0 copy-start.2
  3.0 0.7 copy-done.2
  3.7 0.0 copy-start.3
  3.7 0.7 copy-done.3
  4.3 146.4 %shard_map.59 = (f32[15,2,32,512]{3,2,1,0:T(8,128)S(1)}, f32[6,2,32,512]{3,2,1,0:T(8,128)S(1)}) custom-call(bf16[15,2,32,512]{3,2,1,0:T(8,128)(2,1)S(1)} %copy-done, f32[6,2,32,512]{3,2,1,0:T(8,128)S(1)} %copy-done.1, s32[5,32]{1,0:T(8,128)S(1)} %copy-done.2, s32[6,32]{1,0:T(8,128)S(1)} %copy-done.3), custom_call_target="tpu_custom_call" | custom-call | tf_op jit(solution)/shard_map/pallas_call | solution.py:436
  150.7 1.3 copy.8
  152.0 0.9 copy.9
Async XLA Ops:
  0.6 1.2 copy-start
  1.8 1.1 copy-start.1
  3.0 0.7 copy-start.2
  3.7 0.7 copy-start.3

commit v5 on v4

--- a/solution.py
+++ b/solution.py
@@ -15,9 +15,31 @@
 
 POWER = 6
 PREPARE = ((2, 0), (1, 1), (2, 1), (1, 2), (2, 2), (1, 3), (2, 3), (3, 0), (1, 4))
-BEFORE = {1: (), 2: ((3, 3), (4, 0)), 3: ((4, 2),), 4: ((4, 4), (5, 1)), 5: ((5, 4),)}
-MIDDLE = {1: ((2, 4), (3, 1)), 2: ((3, 4), (4, 1)), 3: ((4, 3), (5, 0)), 4: ((5, 2), (5, 3)), 5: ()}
-AFTER = {1: ((3, 2),), 2: (), 3: (), 4: (), 5: ()}
+BEFORE = {
+    1: (),
+    2: ((3, 3), (4, 0)),
+    3: ((4, 2),),
+    4: ((4, 4), (5, 1, (0,)), (5, 0, (1,))),
+    5: ((5, 4, (0,)), (5, 3, (1,))),
+}
+FIRST = {
+    1: (("pass", 0, 1),),
+    2: (("pass", 1, 1), ("pass", 0, 4)),
+    3: (("pass", 2, 1),),
+    4: (("pass", 3, 1),),
+    5: (),
+}
+BETWEEN = ((5, 4, (1,)),)
+MIDDLE = {
+    1: (("pass", 0, 2), (2, 4), (3, 1)),
+    2: (("pass", 1, 2), (3, 4), (4, 1)),
+    3: (("pass", 2, 2), (4, 3), (5, 0, (0,))),
+    4: ((5, 2, (0,)), (5, 1, (1,)), (5, 3, (0,)), (5, 2, (1,))),
+    5: (),
+}
+AFTER = {1: (("pass", 0, 3), (3, 2)), 2: (("pass", 1, 3),), 3: (), 4: (), 5: ()}
+HOPS = tuple((level, k) for level in range(5) for k in range(6 - level))
+SENDS = tuple((level, k) for level in range(5) for k in range(5 - level))
 
 
 def joint(level):
@@ -46,15 +68,15 @@
 
 
 def kernel(rows_n, cols_n, panel, diag, parents, sizes, cross_out, marg_out, *scratch):
-    cands = scratch[0:5]
-    fulls = scratch[5:10]
-    turn_out = scratch[10:15]
-    turn_in = scratch[15:20]
-    scales = scratch[20:25]
+    fulls = scratch[0:5]
+    turn_out = scratch[5:10]
+    turn_in = scratch[10:15]
+    blocks = {place: scratch[15 + at] for at, place in enumerate(HOPS)}
+    marks = {place: scratch[15 + len(HOPS) + at] for at, place in enumerate(HOPS)}
     (
         lhs, opened, turned_f32, mark_out, mark_in, factor_send, ring_recv, mate_recv,
         chain_send, chain_recv, scale_send, scale_recv, turn_send, turn_recv, mark_send, mark_recv,
-    ) = scratch[25:]
+    ) = scratch[15 + 2 * len(HOPS) :]
     width = diag.shape[3]
     lines = diag.shape[2]
     chips = cols_n // 2
@@ -139,8 +161,8 @@
 
         lax.fori_loop(0, 2, one, 0)
 
-    def ring(level, step):
-        for n in (0, 1):
+    def ring(level, step, nodes=(0, 1)):
+        for n in nodes:
             came = [way for way in (0, 1) if step > 0 and goes(n, way, step - 1)]
             if came:
                 factor_wait(
@@ -154,50 +176,53 @@
             for way in came:
                 mate_copy(level, n, way, step - 1).start()
 
-    def ring_end(level):
-        for n in (0, 1):
-            factor_wait(
-                level, n * level, level, 8, factor_send.at[level - 1], mate_recv.at[level - 1, n]
-            ).wait_recv()
+    def ring_end(level, n):
+        factor_wait(
+            level, n * level, level, 8, factor_send.at[level - 1], mate_recv.at[level - 1, n]
+        ).wait_recv()
 
     def ring_sent(level):
         factor_wait(
             level, 0, 2 * level, 15, factor_send.at[level - 1], mate_recv.at[level - 1, 0]
         ).wait_send()
 
-    def chain_part(level, n, part, there):
-        d = level
-        first, count = ((0, d * d), (d * d, d), (d * d + d, d), (d * d + 2 * d, 1))[part]
-        return cands[d].at[n + 2 if there else n, pl.ds(first, count)]
-
     def remote(src, dst, send, recv, place):
         return pltpu.make_async_remote_copy(
             src_ref=src, dst_ref=dst, send_sem=send, recv_sem=recv, device_id=place, device_id_type=MESH
         )
 
-    def scale_part(level, n, part):
-        first, count = (0, 3 * level) if part == 0 else (3 * level + part - 1, 1)
-        if level == 0:
-            first, count = 0, 3
-        return scales[level].at[n, pl.ds(first, count)]
-
     def pass_on(level, n, part):
-        place = (next_row, col)
+        place, at = (next_row, col), SENDS.index((level, 0))
+        mark = pl.ds(0, 3) if level == 0 else pl.ds(part, 1)
+        span = (pl.ds(0, level), pl.ds(level, level), pl.ds(2 * level, 1))[part]
+        here, there = (level, 0), (level, 1)
         remote(
-            scale_part(level, n, part), scale_part(level, n + 2, part),
-            scale_send.at[level], scale_recv.at[level], place,
+            marks[here].at[n, mark], marks[there].at[n, mark], scale_send.at[at], scale_recv.at[at], place
         ).start()
         remote(
-            chain_part(level, n, part, False), chain_part(level, n, part, True),
-            chain_send.at[level], chain_recv.at[level], place,
+            blocks[here].at[n, span], blocks[there].at[n, span], chain_send.at[at], chain_recv.at[at], place
         ).start()
 
-    def chain_all(level):
-        ours, theirs, place = pl.ds(0, 2), pl.ds(2, 2), (next_row, col)
+    def hop(level, k):
+        place, at = (next_row, col), SENDS.index((level, k))
+        here, there = (level, k), (level, k + 1)
         return (
-            remote(scales[level].at[ours], scales[level].at[theirs], scale_send.at[level], scale_recv.at[level], place),
-            remote(cands[level].at[ours], cands[level].at[theirs], chain_send.at[level], chain_recv.at[level], place),
-        )
+            remote(marks[here], marks[there], scale_send.at[at], scale_recv.at[at], place),
+            remote(blocks[here], blocks[there], chain_send.at[at], chain_recv.at[at], place),
+        )
+
+    arrived = set()
+
+    def receive(level, k):
+        if (level, k) not in arrived:
+            arrived.add((level, k))
+            for copy in hop(level, k - 1):
+                copy.wait_recv()
+
+    def forward(level, k):
+        receive(level, k)
+        for copy in hop(level, k):
+            copy.start()
 
     def turn_copies(level, slab, k):
         there = (col + k) % cols_n
@@ -222,9 +247,6 @@
             remote(pieces, pieces, turn_send.at[level - 1, slab], turn_recv.at[level - 1, slab], place),
         )
 
-    def parts_of(level):
-        return (3,) if level == 0 else (0, 1, 2, 3)
-
     def split(value):
         high = value.astype(BF16)
         return high, (value - high.astype(F32)).astype(BF16)
@@ -236,38 +258,40 @@
     def wide(scale):
         return jnp.concatenate([scale] * (width // 128), axis=1)
 
-    def select_and_cross(level):
-        d = level - 1
+    def select_and_cross(level, nodes):
         start = level * (level - 1) // 2
         tall = lines * level
 
         def one(n, _):
-            node = row * 2 + n
-            parent = parents[d, node]
-            own = (parent >= row * 2) & (parent < row * 2 + 2)
-            slot = jnp.where(own, 0, 2) + lax.rem(parent, 2)
-            table = scales[d][slot]
-            if level < LEVELS - 1:
-                scales[level][n, 0 : 3 * level] = table
+            above = row * 2 + n
+            within, distance = [None] * level, [None] * level
+            for up in range(level - 1, -1, -1):
+                above = parents[up, above]
+                within[up] = lax.rem(above, 2)
+                distance[up] = lax.rem(row + rows_n - lax.div(above, 2), rows_n)
+
+            def pick(refs, up, entry):
+                value = None
+                for k in range(level - up + 1):
+                    ref = refs[(up, k)]
+                    there = ref[within[up]] if entry is None else ref[within[up], entry]
+                    value = there if value is None else lax.select(distance[up] == k, there, value)
+                return value
+
+            table = [pick(marks, up, None) for up in range(level)]
             for l in range(level):
                 for m in range(level):
-                    if l < d and m < d:
-                        entry = l * d + m
-                    elif l < d:
-                        entry = d * d + l
-                    elif m < d:
-                        entry = d * d + d + m
+                    up = max(l, m)
+                    if l == m:
+                        entry, which = 2 * up, 2
+                    elif l < m:
+                        entry, which = l, 0
                     else:
-                        entry = d * d + 2 * d
-                    scale = table[3 * max(l, m) + (2 if l == m else 0 if l < m else 1)]
-                    code = cands[d][slot, entry]
-                    if level < LEVELS - 1:
-                        cands[level][n, l * level + m] = code
-                    high, low = split(decode(code.astype(F32)) * wide(scale))
+                        entry, which = up + m, 1
+                    code = pick(blocks, up, entry)
+                    high, low = split(decode(code.astype(F32)) * wide(table[up][which]))
                     lhs[l * lines : (l + 1) * lines, m * width : (m + 1) * width] = high
                     lhs[tall + l * lines : tall + (l + 1) * lines, m * width : (m + 1) * width] = low
-            if level < LEVELS - 1:
-                pass_on(level, n, 0)
             both = jnp.dot(
                 lhs[0 : 2 * tall, 0 : level * width],
                 fulls[level - 1][pl.ds(n * level, level)].reshape(level * width, width),
@@ -279,10 +303,10 @@
             for l in range(level):
                 cross_out[start + l, n] = crossed[l * lines : (l + 1) * lines, :]
                 if level < LEVELS - 1:
-                    cands[level][n, level * level + l] = code[l * lines : (l + 1) * lines, :].astype(BF16)
+                    blocks[(level, 0)][n, l] = code[l * lines : (l + 1) * lines, :].astype(BF16)
             if level < LEVELS - 1:
-                scales[level][n, 3 * level] = jnp.broadcast_to(scale, (1, 128))
-                pass_on(level, n, 1)
+                marks[(level, 0)][n, 0] = jnp.broadcast_to(scale, (1, 128))
+                pass_on(level, n, 0)
             turned = jnp.transpose(code, (1, 0)).astype(BF16)
             slab = 0 if joint(level) else n
             first = n * tall if joint(level) else 0
@@ -303,6 +327,8 @@
             one(0, 0)
             one(1, 0)
             send_turn(level, 0)
+        elif len(nodes) == 1:
+            one(nodes[0], 0)
         else:
             lax.fori_loop(0, 2, one, 0)
 
@@ -355,9 +381,9 @@
                 scale = scale_of(whole)
                 code = encode(whole, scale).astype(BF16)
                 for l in range(level):
-                    cands[level][n, level * level + level + l] = code[l * lines : (l + 1) * lines, :]
-                scales[level][n, 3 * level + 1] = jnp.broadcast_to(scale, (1, 128))
-                pass_on(level, n, 2)
+                    blocks[(level, 0)][n, level + l] = code[l * lines : (l + 1) * lines, :]
+                marks[(level, 0)][n, 1] = jnp.broadcast_to(scale, (1, 128))
+                pass_on(level, n, 1)
             both = jnp.dot(
                 lhs[0 : 2 * lines, 0 : level * width],
                 fulls[level - 1][pl.ds(n * level, level)].reshape(level * width, width),
@@ -378,13 +404,13 @@
 
     def keep_marginal(level, n, marginal):
         scale = scale_of(marginal)
-        cands[level][n, level * level + 2 * level] = encode(marginal, scale).astype(BF16)
-        for entry in range(3) if level == 0 else (3 * level + 2,):
-            scales[level][n, entry] = jnp.broadcast_to(scale, (1, 128))
+        blocks[(level, 0)][n, 2 * level] = encode(marginal, scale).astype(BF16)
+        for entry in range(3) if level == 0 else (2,):
+            marks[(level, 0)][n, entry] = jnp.broadcast_to(scale, (1, 128))
 
     def send_marginal(level, n, marginal):
         keep_marginal(level, n, marginal)
-        pass_on(level, n, 3)
+        pass_on(level, n, 2)
 
     mask_factor(1)
     for n in range(2):
@@ -395,29 +421,43 @@
         mask_factor(level)
     pl.semaphore_wait(barrier, cols_n + 1)
     ring(1, 0)
-    pass_on(0, 0, 3)
-    pass_on(0, 1, 3)
-    for job in PREPARE:
-        ring(*job)
+    pass_on(0, 0, 2)
+    pass_on(0, 1, 2)
+
+    def run(jobs):
+        for job in jobs:
+            if job[0] == "pass":
+                forward(*job[1:])
+            else:
+                ring(*job)
+
+    run(PREPARE)
     for level in range(1, LEVELS):
-        for job in BEFORE[level]:
-            ring(*job)
-        ring_end(level)
-        for copy in chain_all(level - 1):
-            copy.wait_recv()
-        select_and_cross(level)
-        for job in MIDDLE[level]:
-            ring(*job)
+        run(BEFORE[level])
+        for up in range(level - 1, -1, -1):
+            receive(up, level - up)
+        run(FIRST[level])
+        if level < LEVELS - 1:
+            ring_end(level, 0)
+            ring_end(level, 1)
+            select_and_cross(level, (0, 1))
+        else:
+            ring_end(level, 0)
+            select_and_cross(level, (0,))
+            run(BETWEEN)
+            ring_end(level, 1)
+            select_and_cross(level, (1,))
+        run(MIDDLE[level])
         finish_level(level)
-        for job in AFTER[level]:
-            ring(*job)
+        run(AFTER[level])
 
     for level in range(1, LEVELS):
         ring_sent(level)
         for slab in (0,) if joint(level) else (0, 1):
             for copy in turn_all(level, slab):
                 copy.wait_send()
-        for copy in chain_all(level - 1):
+    for level, k in SENDS:
+        for copy in hop(level, k):
             copy.wait_send()
 
 
@@ -442,11 +482,11 @@
             in_specs=[vmem, vmem, smem, smem],
             out_specs=(vmem, vmem),
             scratch_shapes=[
-                *[pltpu.VMEM((4, (d + 1) * (d + 1), lines, width), BF16) for d in range(5)],
                 *[pltpu.VMEM((2 * d, width, width), BF16) for d in range(1, 6)],
                 *[pltpu.VMEM(turn_shape(d), BF16) for d in range(1, 6)],
                 *[pltpu.VMEM(turn_shape(d), BF16) for d in range(1, 6)],
-                *[pltpu.VMEM((4, 3 * (d + 1), 1, 128), F32) for d in range(5)],
+                *[pltpu.VMEM((per, 2 * level + 1, lines, width), BF16) for level, _ in HOPS],
+                *[pltpu.VMEM((per, 3, 1, 128), F32) for _ in HOPS],
                 pltpu.VMEM((320, 5 * width), BF16),
                 pltpu.VMEM((cols_n, lines, 256), F32),
                 pltpu.VMEM((4 * lines, width), F32),
@@ -455,10 +495,10 @@
                 dma((5,)),
                 dma((5, 2, 4)),
                 dma((5, 2)),
-                dma((5,)),
-                dma((5,)),
-                dma((5,)),
-                dma((5,)),
+                dma((len(SENDS),)),
+                dma((len(SENDS),)),
+                dma((len(SENDS),)),
+                dma((len(SENDS),)),
                 dma((5, 2)),
                 dma((5, 2)),
                 dma((5, 2)),

time: 153 us -> 148 us (0.967)
  Pallas kernels: 146 us -> 141 us
    pallas_call x1, Pallas kernels: 146 us -> 141 us  [shards(): pl.pallas_call(functools.partial(kernel, rows_n, cols_n), out_shape=(jax....]
where the time goes in v5:
time: 148 us
  Pallas kernels  141 us (95%)
  local copies, waits for them, and re-layouts  5.85 us (4%)
    pallas_call x1, Pallas kernels, shards(): pl.pallas_call(functools.partial(kernel, rows_n, cols_n), out_shape=(jax....  141 us
    unnamed x10, local copies, waits for them, and re-layouts  5.85 us

profile of v5, /device:TPU:1, one launch (start us, length us, event | category | flops | bytes accessed | tf_op | source)
XLA Modules:
  0.0 147.7 jit_solution(7984118535148972204)
XLA Ops:
  0.6 0.0 copy-start
  0.6 1.2 copy-done
  1.8 0.0 copy-start.1
  1.8 1.1 copy-done.1
  3.0 0.0 copy-start.2
  3.0 0.7 copy-done.2
  3.7 0.0 copy-start.3
  3.7 0.7 copy-done.3
  4.3 141.2 %shard_map.59 = (f32[15,2,32,512]{3,2,1,0:T(8,128)S(1)}, f32[6,2,32,512]{3,2,1,0:T(8,128)S(1)}) custom-call(bf16[15,2,32,512]{3,2,1,0:T(8,128)(2,1)S(1)} %copy-done, f32[6,2,32,512]{3,2,1,0:T(8,128)S(1)} %copy-done.1, s32[5,32]{1,0:T(8,128)S(1)} %copy-done.2, s32[6,32]{1,0:T(8,128)S(1)} %copy-done.3), custom_call_target="tpu_custom_call" | custom-call | tf_op jit(solution)/shard_map/pallas_call | solution.py:476
  145.5 1.3 copy.8
  146.8 0.9 copy.9
Async XLA Ops:
  0.6 1.2 copy-start
  1.8 1.1 copy-start.1
  3.0 0.7 copy-start.2
  3.7 0.7 copy-start.3

commit v6 on v5

--- a/solution.py
+++ b/solution.py
@@ -15,29 +15,11 @@
 
 POWER = 6
 PREPARE = ((2, 0), (1, 1), (2, 1), (1, 2), (2, 2), (1, 3), (2, 3), (3, 0), (1, 4))
-BEFORE = {
-    1: (),
-    2: ((3, 3), (4, 0)),
-    3: ((4, 2),),
-    4: ((4, 4), (5, 1, (0,)), (5, 0, (1,))),
-    5: ((5, 4, (0,)), (5, 3, (1,))),
-}
-FIRST = {
-    1: (("pass", 0, 1),),
-    2: (("pass", 1, 1), ("pass", 0, 4)),
-    3: (("pass", 2, 1),),
-    4: (("pass", 3, 1),),
-    5: (),
-}
+BEFORE = {1: (), 2: ((4, 1), (3, 3)), 3: ((4, 3), (5, 1, (0,))), 4: ((5, 1, (1,)), (5, 3, (0,))), 5: ()}
+FIRST = {1: (('pass', 0, 1),), 2: (('pass', 1, 1), ('pass', 0, 4)), 3: (('pass', 2, 1),), 4: (('pass', 3, 1),), 5: ()}
 BETWEEN = ((5, 4, (1,)),)
-MIDDLE = {
-    1: (("pass", 0, 2), (2, 4), (3, 1)),
-    2: (("pass", 1, 2), (3, 4), (4, 1)),
-    3: (("pass", 2, 2), (4, 3), (5, 0, (0,))),
-    4: ((5, 2, (0,)), (5, 1, (1,)), (5, 3, (0,)), (5, 2, (1,))),
-    5: (),
-}
-AFTER = {1: (("pass", 0, 3), (3, 2)), 2: (("pass", 1, 3),), 3: (), 4: (), 5: ()}
+MIDDLE = {1: (('pass', 0, 2), (2, 4), (3, 1), (4, 0)), 2: (('pass', 1, 2), (4, 2), (3, 4)), 3: (('pass', 2, 2), (5, 0, (1,)), (4, 4)), 4: ((5, 2, (1,)), (5, 4, (0,))), 5: ()}
+AFTER = {1: (('pass', 0, 3), (3, 2)), 2: (('pass', 1, 3), (5, 0, (0,))), 3: ((5, 2, (0,)),), 4: ((5, 3, (1,)),), 5: ()}
 HOPS = tuple((level, k) for level in range(5) for k in range(6 - level))
 SENDS = tuple((level, k) for level in range(5) for k in range(5 - level))
 
@@ -91,8 +73,8 @@
     prev_row = (row + rows_n - 1) % rows_n
 
     barrier = pltpu.get_barrier_semaphore()
-    for k in range(1, cols_n):
-        pl.semaphore_signal(barrier, inc=1, device_id=(row, (col + k) % cols_n), device_id_type=MESH)
+    for peer in (right, left, mate):
+        pl.semaphore_signal(barrier, inc=1, device_id=(row, peer), device_id_type=MESH)
     pl.semaphore_signal(barrier, inc=1, device_id=(next_row, col), device_id_type=MESH)
     pl.semaphore_signal(barrier, inc=1, device_id=(prev_row, col), device_id_type=MESH)
     line_of = lax.broadcasted_iota(jnp.int32, (lines, width), 0) + col * lines
@@ -419,7 +401,7 @@
         keep_marginal(0, n, marginal)
     for level in range(2, LEVELS):
         mask_factor(level)
-    pl.semaphore_wait(barrier, cols_n + 1)
+    pl.semaphore_wait(barrier, 5)
     ring(1, 0)
     pass_on(0, 0, 2)
     pass_on(0, 1, 2)

time: 148 us -> 145 us (0.980)
  Pallas kernels: 141 us -> 138 us
    pallas_call x1, Pallas kernels: 141 us -> 138 us  [shards(): pl.pallas_call(functools.partial(kernel, rows_n, cols_n), out_shape=(jax....]
where the time goes in v6:
time: 145 us
  Pallas kernels  138 us (95%)
  local copies, waits for them, and re-layouts  5.85 us (4%)
    pallas_call x1, Pallas kernels, shards(): pl.pallas_call(functools.partial(kernel, rows_n, cols_n), out_shape=(jax....  138 us
    unnamed x10, local copies, waits for them, and re-layouts  5.85 us

profile of v6, /device:TPU:1, one launch (start us, length us, event | category | flops | bytes accessed | tf_op | source)
XLA Modules:
  0.0 144.6 jit_solution(12922160935962047673)
XLA Ops:
  0.6 0.0 copy-start
  0.6 1.2 copy-done
  1.8 0.0 copy-start.1
  1.8 1.1 copy-done.1
  3.0 0.0 copy-start.2
  3.0 0.7 copy-done.2
  3.7 0.0 copy-start.3
  3.7 0.7 copy-done.3
  4.3 138.1 %shard_map.59 = (f32[15,2,32,512]{3,2,1,0:T(8,128)S(1)}, f32[6,2,32,512]{3,2,1,0:T(8,128)S(1)}) custom-call(bf16[15,2,32,512]{3,2,1,0:T(8,128)(2,1)S(1)} %copy-done, f32[6,2,32,512]{3,2,1,0:T(8,128)S(1)} %copy-done.1, s32[5,32]{1,0:T(8,128)S(1)} %copy-done.2, s32[6,32]{1,0:T(8,128)S(1)} %copy-done.3), custom_call_target="tpu_custom_call" | custom-call | tf_op jit(solution)/shard_map/pallas_call | solution.py:458
  142.5 1.3 copy.8
  143.7 0.9 copy.9
Async XLA Ops:
  0.6 1.2 copy-start
  1.8 1.1 copy-start.1
  3.0 0.7 copy-start.2
  3.7 0.7 copy-start.3

commit v7 on v6

--- a/solution.py
+++ b/solution.py
@@ -28,9 +28,8 @@
     return level <= 2
 
 
-def lanes_of(level):
-    tall = 32 * level * (2 if joint(level) else 1)
-    return 128 * (-(-tall // 128))
+def slabs_of(level):
+    return 1 if joint(level) else 2 if level < 5 else 3
 
 
 def scale_of(value):
@@ -293,14 +292,21 @@
             slab = 0 if joint(level) else n
             first = n * tall if joint(level) else 0
             for c in range(cols_n):
-                turn_out[level - 1][slab, c, :, first : first + tall] = turned[
-                    c * lines : (c + 1) * lines, :
-                ]
+                piece = turned[c * lines : (c + 1) * lines, :]
+                turn_out[level - 1][slab, c, :, first : first + min(tall, 128)] = piece[:, 0:128]
+                if tall > 128:
+                    turn_out[level - 1][2, c, :, n * lines : (n + 1) * lines] = piece[:, 128:tall]
             lane = lax.broadcasted_iota(jnp.int32, (1, 128), 1)
             mark = jnp.broadcast_to(scale, (1, 128))
             if joint(level) and n == 1:
                 mark = jnp.where(lane < tall, mark_out[level - 1, 0], mark)
             mark_out[level - 1, slab] = mark
+            if tall > 128:
+                if n == 1:
+                    mark = jnp.where(lane < lines, mark_out[level - 1, 2], mark)
+                mark_out[level - 1, 2] = mark
+                if n == 1:
+                    send_turn(level, 2)
             if not joint(level):
                 send_turn(level, n)
             return 0
@@ -327,12 +333,11 @@
     def open_turn(level, slab):
         for copy in turn_all(level, slab):
             copy.wait_recv()
-        lanes = lanes_of(level)
+        place = 128 if slabs_of(level) == 3 and slab == 2 else 0
 
         def undo(c, _):
             code = turn_in[level - 1][slab, c].astype(F32)
-            mark = jnp.concatenate([mark_in[level - 1, slab, c]] * (lanes // 128), axis=1)
-            opened[c, :, 0:lanes] = decode(code) * mark
+            opened[c, :, place : place + 128] = decode(code) * mark_in[level - 1, slab, c]
             return 0
 
         lax.fori_loop(0, cols_n, undo, 0)
@@ -340,9 +345,11 @@
     def finish_level(level):
         def one(n, _):
             if not joint(level):
+                if slabs_of(level) == 3 and n == 0:
+                    open_turn(level, 2)
                 open_turn(level, n)
             for l in range(level):
-                group = l + n * level if joint(level) else l
+                group = l + n * level if joint(level) else l if l < 4 else 4 + n
                 for q in range(width // 128):
                     piece = None
                     for k in range(per):
@@ -381,8 +388,11 @@
             open_turn(level, 0)
             one(0, 0)
             one(1, 0)
+        elif slabs_of(level) == 2:
+            lax.fori_loop(0, 2, one, 0)
         else:
-            lax.fori_loop(0, 2, one, 0)
+            one(0, 0)
+            one(1, 0)
 
     def keep_marginal(level, n, marginal):
         scale = scale_of(marginal)
@@ -435,7 +445,7 @@
 
     for level in range(1, LEVELS):
         ring_sent(level)
-        for slab in (0,) if joint(level) else (0, 1):
+        for slab in range(slabs_of(level)):
             for copy in turn_all(level, slab):
                 copy.wait_send()
     for level, k in SENDS:
@@ -453,7 +463,7 @@
         dma = pltpu.SemaphoreType.DMA
 
         def turn_shape(level):
-            return (1 if joint(level) else 2, cols_n, lines, lanes_of(level))
+            return (slabs_of(level), cols_n, lines, 128)
 
         return pl.pallas_call(
             functools.partial(kernel, rows_n, cols_n),
@@ -472,8 +482,8 @@
                 pltpu.VMEM((320, 5 * width), BF16),
                 pltpu.VMEM((cols_n, lines, 256), F32),
                 pltpu.VMEM((4 * lines, width), F32),
-                pltpu.VMEM((5, 2, 1, 128), F32),
-                pltpu.VMEM((5, 2, cols_n, 1, 128), F32),
+                pltpu.VMEM((5, 3, 1, 128), F32),
+                pltpu.VMEM((5, 3, cols_n, 1, 128), F32),
                 dma((5,)),
                 dma((5, 2, 4)),
                 dma((5, 2)),
@@ -481,10 +491,10 @@
                 dma((len(SENDS),)),
                 dma((len(SENDS),)),
                 dma((len(SENDS),)),
-                dma((5, 2)),
-                dma((5, 2)),
-                dma((5, 2)),
-                dma((5, 2)),
+                dma((5, 3)),
+                dma((5, 3)),
+                dma((5, 3)),
+                dma((5, 3)),
             ],
             compiler_params=pltpu.CompilerParams(
                 collective_id=0, has_side_effects=True, vmem_limit_bytes=44000 * 1024

time: 145 us -> 144 us (level)
  no operation moved by 1% of the time
where the time goes in v7:
time: 144 us
  Pallas kernels  137 us (95%)
  local copies, waits for them, and re-layouts  5.85 us (4%)
    pallas_call x1, Pallas kernels, shards(): pl.pallas_call(functools.partial(kernel, rows_n, cols_n), out_shape=(jax....  137 us
    unnamed x10, local copies, waits for them, and re-layouts  5.85 us

profile of v7, /device:TPU:1, one launch (start us, length us, event | category | flops | bytes accessed | tf_op | source)
XLA Modules:
  0.0 143.8 jit_solution(6097658870490189722)
XLA Ops:
  0.6 0.0 copy-start
  0.6 1.2 copy-done
  1.8 0.0 copy-start.1
  1.8 1.1 copy-done.1
  3.0 0.0 copy-start.2
  3.0 0.7 copy-done.2
  3.7 0.0 copy-start.3
  3.7 0.7 copy-done.3
  4.3 137.3 %shard_map.59 = (f32[15,2,32,512]{3,2,1,0:T(8,128)S(1)}, f32[6,2,32,512]{3,2,1,0:T(8,128)S(1)}) custom-call(bf16[15,2,32,512]{3,2,1,0:T(8,128)(2,1)S(1)} %copy-done, f32[6,2,32,512]{3,2,1,0:T(8,128)S(1)} %copy-done.1, s32[5,32]{1,0:T(8,128)S(1)} %copy-done.2, s32[6,32]{1,0:T(8,128)S(1)} %copy-done.3), custom_call_target="tpu_custom_call" | custom-call | tf_op jit(solution)/shard_map/pallas_call | solution.py:468
  141.6 1.3 copy.8
  142.9 0.9 copy.9
Async XLA Ops:
  0.6 1.2 copy-start
  1.8 1.1 copy-start.1
  3.0 0.7 copy-start.2
  3.7 0.7 copy-start.3

commit v8 on v7

--- a/solution.py
+++ b/solution.py
@@ -14,12 +14,12 @@
 
 
 POWER = 6
-PREPARE = ((2, 0), (1, 1), (2, 1), (1, 2), (2, 2), (1, 3), (2, 3), (3, 0), (1, 4))
-BEFORE = {1: (), 2: ((4, 1), (3, 3)), 3: ((4, 3), (5, 1, (0,))), 4: ((5, 1, (1,)), (5, 3, (0,))), 5: ()}
+PREPARE = ((2, 0), (1, 1), (2, 1), (1, 2), (2, 2), (1, 3), (1, 4))
+BEFORE = {1: (), 2: ((3, 2),), 3: ((4, 2),), 4: (), 5: ()}
 FIRST = {1: (('pass', 0, 1),), 2: (('pass', 1, 1), ('pass', 0, 4)), 3: (('pass', 2, 1),), 4: (('pass', 3, 1),), 5: ()}
 BETWEEN = ((5, 4, (1,)),)
-MIDDLE = {1: (('pass', 0, 2), (2, 4), (3, 1), (4, 0)), 2: (('pass', 1, 2), (4, 2), (3, 4)), 3: (('pass', 2, 2), (5, 0, (1,)), (4, 4)), 4: ((5, 2, (1,)), (5, 4, (0,))), 5: ()}
-AFTER = {1: (('pass', 0, 3), (3, 2)), 2: (('pass', 1, 3), (5, 0, (0,))), 3: ((5, 2, (0,)),), 4: ((5, 3, (1,)),), 5: ()}
+MIDDLE = {1: (('pass', 0, 2), (2, 3), (3, 0)), 2: (('pass', 1, 2), (3, 3), (4, 0)), 3: (('pass', 2, 2), (4, 3), (5, 0, (0,))), 4: ((5, 2, (0,)), (5, 1, (1,)), (5, 3, (0,))), 5: ()}
+AFTER = {1: (('pass', 0, 3), (2, 4), (3, 1)), 2: (('pass', 1, 3), (3, 4), (4, 1)), 3: ((4, 4), (5, 1, (0,)), (5, 0, (1,))), 4: ((5, 2, (1,)), (5, 4, (0,)), (5, 3, (1,))), 5: ()}
 HOPS = tuple((level, k) for level in range(5) for k in range(6 - level))
 SENDS = tuple((level, k) for level in range(5) for k in range(5 - level))
 

time: 144 us -> 140 us (0.972)
  Pallas kernels: 137 us -> 133 us
    pallas_call x1, Pallas kernels: 137 us -> 133 us  [shards(): pl.pallas_call(functools.partial(kernel, rows_n, cols_n), out_shape=(jax....]
where the time goes in v8:
time: 140 us
  Pallas kernels  133 us (95%)
  local copies, waits for them, and re-layouts  5.85 us (4%)
    pallas_call x1, Pallas kernels, shards(): pl.pallas_call(functools.partial(kernel, rows_n, cols_n), out_shape=(jax....  133 us
    unnamed x10, local copies, waits for them, and re-layouts  5.85 us

profile of v8, /device:TPU:1, one launch (start us, length us, event | category | flops | bytes accessed | tf_op | source)
XLA Modules:
  0.0 139.8 jit_solution(12813240449462862106)
XLA Ops:
  0.6 0.0 copy-start
  0.6 1.2 copy-done
  1.8 0.0 copy-start.1
  1.8 1.1 copy-done.1
  3.0 0.0 copy-start.2
  3.0 0.7 copy-done.2
  3.7 0.0 copy-start.3
  3.7 0.7 copy-done.3
  4.3 133.3 %shard_map.59 = (f32[15,2,32,512]{3,2,1,0:T(8,128)S(1)}, f32[6,2,32,512]{3,2,1,0:T(8,128)S(1)}) custom-call(bf16[15,2,32,512]{3,2,1,0:T(8,128)(2,1)S(1)} %copy-done, f32[6,2,32,512]{3,2,1,0:T(8,128)S(1)} %copy-done.1, s32[5,32]{1,0:T(8,128)S(1)} %copy-done.2, s32[6,32]{1,0:T(8,128)S(1)} %copy-done.3), custom_call_target="tpu_custom_call" | custom-call | tf_op jit(solution)/shard_map/pallas_call | solution.py:468
  137.7 1.3 copy.8
  139.0 0.9 copy.9
Async XLA Ops:
  0.6 1.2 copy-start
  1.8 1.1 copy-start.1
  3.0 0.7 copy-start.2
  3.7 0.7 copy-start.3
